TPU v7x, 512 devices: a whole 4x8x8 slice. The times are simulated.
512 devices in a mesh: slab: 32 (over y_lo, x, core), chan: 16 (over y_hi, z).
Axes of the slice: x: 4, y: 8 (y_hi: 2, y_lo: 4; y = y_hi * 4 + y_lo), z: 8, core: 2. Of those that a mesh axis runs over, the one named last changes fastest.
Arguments:
- inputs: bfloat16 [256, 64, 1536], P('chan', 'slab'), may hold values from -6 to 6
- filters: bfloat16 [27, 256, 256], P(None, 'chan'), may hold values from -0.078125 to 0.078125
- cotangent: bfloat16 [256, 64, 1536], P('chan', 'slab'), may hold values from -6 to 6
Outputs:
- features: bfloat16 [256, 64, 1536], P('chan', 'slab')
- input_grad: bfloat16 [256, 64, 1536], P('chan', 'slab')
- filter_grad: float32 [27, 256, 256], P(None, 'chan', 'slab')
All inputs are finite; a program needn't handle non-finite values.
Results may differ from a plain program's by a relative error of at most 0.001.
Values may be sent and summed in bfloat16 or wider, within the bound.
No kernel may reach another device: no remote copies, remote signals or barrier semaphores. Data moves between devices by JAX's collectives and lax.ppermute only.
A program may use at most 64 MiB of HBM per device.

v0:
```python
import math

import jax
import jax.numpy as jnp
from jax import lax
from jax.sharding import PartitionSpec as P

W = 64


offsets = (-1, 0, 1)


def padded(cells, sides, width):
    for axis, dim in sides:
        count = lax.axis_size(axis)
        head = lax.slice_in_dim(cells, 0, width, axis=dim)
        tail = lax.slice_in_dim(cells, cells.shape[dim] - width, cells.shape[dim], axis=dim)
        cells = jnp.concatenate(
            [
                lax.ppermute(tail, axis, [(i, (i + 1) % count) for i in range(count)]),
                cells,
                lax.ppermute(head, axis, [((i + 1) % count, i) for i in range(count)]),
            ],
            axis=dim,
        )
    return cells


def roll_cells(values, row_shift, column_shift):
    row_width = W
    length = values.shape[-1]
    column = lax.broadcasted_iota(jnp.int32, (length,), 0) % row_width
    if column_shift == 1:
        values = jnp.where(
            column == 0, jnp.roll(values, 1 - row_width, axis=-1), jnp.roll(values, 1, axis=-1)
        )
    elif column_shift == -1:
        values = jnp.where(
            column == row_width - 1,
            jnp.roll(values, row_width - 1, axis=-1),
            jnp.roll(values, -1, axis=-1),
        )
    if row_shift != 0:
        values = jnp.roll(values, row_shift * row_width, axis=-1)
    return values


def add_rims(stacked):
    return padded(stacked, (("slab", 2),), 1)


def local(inputs, filters, cotangent):
    planes = inputs.shape[1]
    flat_cells = inputs.shape[2]
    factor = 1.0 / math.sqrt(planes * lax.axis_size("slab") * flat_cells)
    rimmed = add_rims(jnp.stack([inputs, cotangent]))
    inputs_wide = lax.all_gather(rimmed[0], "chan", axis=0, tiled=True)
    grads_rims = rimmed[1]
    rolled_rims = jnp.stack(
        [
            roll_cells(grads_rims, row_shift, column_shift)
            for row_shift in offsets
            for column_shift in offsets
        ]
    )
    rolled = rolled_rims[:, :, 1 : 1 + planes]
    result = jnp.zeros((filters.shape[1], planes, flat_cells), jnp.float32)
    blocks = []
    for plane_shift in offsets:
        window = inputs_wide[:, plane_shift + 1 : plane_shift + 1 + planes]
        tap_rows = filters[9 * (plane_shift + 1) : 9 * (plane_shift + 2)]
        partial_value = jnp.einsum(
            "koc,cdp->kodp", tap_rows, window, preferred_element_type=jnp.float32
        )
        for row_shift in offsets:
            for column_shift in offsets:
                result = result + roll_cells(
                    partial_value[3 * (row_shift + 1) + column_shift + 1], -row_shift, -column_shift
                )
        blocks.append(
            jnp.einsum("kodp,cdp->koc", rolled, window, preferred_element_type=jnp.float32)
        )
    features = result.astype(jnp.bfloat16)
    filter_local = jnp.concatenate(blocks, 0) * factor
    filter_grad = lax.psum_scatter(filter_local, "slab", scatter_dimension=2, tiled=True)
    stacked = jnp.concatenate(
        [rolled_rims[:, :, 1 - plane_shift : 1 - plane_shift + planes] for plane_shift in offsets],
        0,
    )
    tap_rows = filters
    gradient = lax.psum_scatter(
        jnp.einsum("koc,kodp->cdp", tap_rows, stacked, preferred_element_type=jnp.float32),
        "chan",
        scatter_dimension=0,
        tiled=True,
    )
    input_grad = gradient.astype(jnp.bfloat16)
    return (features, input_grad, filter_grad)


def solution(mesh):
    placed = (P("chan", "slab", None), P(None, "chan", None), P("chan", "slab", None))
    return jax.shard_map(
        local,
        mesh=mesh,
        in_specs=placed,
        out_specs=(P("chan", "slab", None), P("chan", "slab", None), P(None, "chan", "slab")),
        check_vma=False,
    )
```

profile of v0, /device:TPU:64, one launch (start us, length us, event | category | flops | bytes accessed | tf_op | source)
XLA Modules:
  0.0 443.7 jit_solution(11153294252014674681)
XLA Ops:
  7.2 1.0 copy_bitcast_fusion
  8.2 1.9 collective-permute-start
  10.1 7.5 %collective-permute-start.1 = (bf16[2,16,1,1536]{3,1,2,0:T(8,128)(2,1)S(1)}, bf16[2,16,1,1536]{3,1,2,0:T(8,128)(2,1)S(1)}, u32[]{:S(2)}, u32[]{:S(2)}) collective-permute-start(bf16[2,16,1,1536]{3,1,2,0:T(8,128)(2,1)S(1)} %get-tuple-element.70), channel_id=1, source_target_pairs={{16,0},{32,16},{48,32},{64,48},{80,64},{96,80},{112,96},{128,112},... | collective-permute-start | bytes 294920 | tf_op jit(solution)/shard_map/ppermute | solution.py:23
  17.7 1.3 dynamic-slice
  20.2 0.7 slice_bitcast_fusion.38
  20.9 0.6 slice_bitcast_fusion.39
  21.8 0.7 fusion.70
  22.6 0.7 fusion.68
  23.5 0.7 fusion.66
  24.6 0.7 slice_dynamic-update-slice_fusion
  25.4 0.9 fusion.48
  27.0 1.0 copy-done
  28.0 2.8 convolution_bitcast_fusion
  30.8 4.3 copy.58
  35.0 191.2 %all-reduce.2 = bf16[256,2,1536]{2,1,0:T(2,128)(2,1)} all-reduce(f32[256,2,1536]{2,1,0:T(2,128)S(1)} %copy.58), channel_id=3, replica_groups=mesh['slab'=32,'chan'=16] {'chan'}, use_global_device_ids=true, to_apply=%region_0.1.clone | all-reduce | flops 786432 | bytes 4718592
  226.3 1.6 dynamic-slice_convert_fusion
  227.9 2.5 fusion.12
  230.3 0.7 copy-done.19
  231.0 0.6 fusion.13
  231.7 0.6 fusion.14
  233.6 1.1 slice_bitcast_fusion.28
  234.9 0.8 slice_bitcast_fusion.19
  236.1 0.8 slice_bitcast_fusion.10
  237.1 1.0 maximum_select_fusion.17
  238.1 0.8 slice.760
  239.5 0.8 slice.806
  240.8 0.8 slice.852
  243.0 1.0 maximum_select_fusion.16
  244.0 0.8 slice.750
  245.4 0.8 slice.796
  246.8 0.8 slice.842
  248.2 0.8 slice.730
  249.0 0.7 slice.728
  250.3 0.8 slice.822
  251.1 0.7 slice.820
  252.4 0.8 slice.718
  253.8 0.7 slice.720
  254.4 0.8 slice.810
  255.8 0.7 slice.812
  256.5 0.8 slice.735
  257.9 0.7 slice.737
  258.6 0.8 slice.743
  259.4 0.7 slice.741
  260.7 0.8 slice.753
  262.1 0.8 slice.781
  263.5 0.7 slice.783
  264.1 0.8 slice.789
  264.9 0.7 slice.787
  266.2 0.8 slice.799
  267.6 0.8 slice.827
  269.0 0.7 slice.829
  269.7 0.8 slice.835
  270.5 0.7 slice.833
  271.7 0.8 slice.845
  273.1 0.8 maximum_multiply_fusion
  274.0 3.6 copy.59
  277.7 1.0 slice.778
  278.7 0.8 slice.768
  279.5 1.3 maximum_select_fusion.13
  281.0 1.3 maximum_select_fusion.12
  282.8 2.7 fusion.23
  285.5 0.7 copy.60
  286.2 149.2 %reduce-scatter.2.cloned.1.call-done = f32[27,16,8]{0,1,2:T(8,128)} async-done(((f32[27,16,256]{0,1,2:T(8,128)}), f32[27,16,8]{0,1,2:T(8,128)}) %reduce-scatter.2.cloned.1.call-update) | async-done | bytes 13840 | tf_op jit(solution)/shard_map/reduce_scatter | solution.py:86
  435.4 1.5 copy.61
  (136 shorter events, 17.0 us)
Async XLA Ops:
  7.2 220.7 %all-gather.3.cloned.1.call-start = ((), (), s32[]{:S(2)}) async-start(), calls=%async_computation.2 | async-start | bytes 3342336 | tf_op jit(solution)/shard_map/all_gather | solution.py:58
  8.2 11.4 %collective-permute-start = (bf16[2,16,1,1536]{3,1,2,0:T(8,128)(2,1)S(1)}, bf16[2,16,1,1536]{3,1,2,0:T(8,128)(2,1)S(1)}, u32[]{:S(2)}, u32[]{:S(2)}) collective-permute-start(bf16[2,16,1,1536]{3,1,2,0:T(8,128)(2,1)S(1)} %get-tuple-element.69), channel_id=1, source_target_pairs={{0,16},{16,32},{32,48},{48,64},{64,80},{80,96},{96,112},{112,128},... | collective-permute-start | bytes 294920 | tf_op jit(solution)/shard_map/ppermute | solution.py:21
  10.1 9.7 %collective-permute-start.1 = (bf16[2,16,1,1536]{3,1,2,0:T(8,128)(2,1)S(1)}, bf16[2,16,1,1536]{3,1,2,0:T(8,128)(2,1)S(1)}, u32[]{:S(2)}, u32[]{:S(2)}) collective-permute-start(bf16[2,16,1,1536]{3,1,2,0:T(8,128)(2,1)S(1)} %get-tuple-element.70), channel_id=1, source_target_pairs={{16,0},{32,16},{48,32},{64,48},{80,64},{96,80},{112,96},{128,112},... | collective-permute-start | bytes 294920 | tf_op jit(solution)/shard_map/ppermute | solution.py:23
  24.2 2.1 copy-start.25
  24.3 2.1 copy-start.26
  24.4 2.2 copy-start.27
  25.3 410.0 %reduce-scatter.2.cloned.1.call-start = ((), (), s32[]{:S(2)}) async-start(), calls=%async_computation.1 | async-start | bytes 2162688 | tf_op jit(solution)/shard_map/reduce_scatter | solution.py:86
  26.7 1.3 copy-start
  26.7 1.3 copy-start.28
  227.9 2.5 copy-start.1
  227.9 3.2 copy-start.19
  233.1 1.7 copy-start.3
  233.5 2.6 copy-start.4
  236.9 14.8 %copy-start.2 = (f32[16,2,1536]{2,0,1:T(8,128)}, f32[16,2,1536]{2,0,1:T(8,128)S(1)}, u32[]{:S(2)}) copy-start(f32[16,2,1536]{2,0,1:T(8,128)S(1)} %get-tuple-element.20) | copy-start | bytes 589828
  277.5 4.9 %copy-start.5 = (f32[16,2,1536]{2,0,1:T(8,128)S(1)}, f32[16,2,1536]{2,0,1:T(8,128)}, u32[]{:S(2)}) copy-start(f32[16,2,1536]{2,0,1:T(8,128)} %get-tuple-element.36) | copy-start | bytes 589828
  277.6 4.9 %copy-start.6 = (f32[16,2,1536]{2,0,1:T(8,128)S(1)}, f32[16,2,1536]{2,0,1:T(8,128)}, u32[]{:S(2)}) copy-start(f32[16,2,1536]{2,0,1:T(8,128)} %get-tuple-element.29) | copy-start | bytes 589828
  277.6 5.0 %copy-start.7 = (f32[16,2,1536]{2,0,1:T(8,128)S(1)}, f32[16,2,1536]{2,0,1:T(8,128)}, u32[]{:S(2)}) copy-start(f32[16,2,1536]{2,0,1:T(8,128)} %get-tuple-element.21) | copy-start | bytes 589828
  277.6 5.1 %copy-start.8 = (f32[16,2,1536]{2,0,1:T(8,128)S(1)}, f32[16,2,1536]{2,0,1:T(8,128)}, u32[]{:S(2)}) copy-start(f32[16,2,1536]{2,0,1:T(8,128)} %get-tuple-element.73) | copy-start | bytes 589828
  277.6 5.0 %copy-start.9 = (f32[16,2,1536]{2,0,1:T(8,128)S(1)}, f32[16,2,1536]{2,0,1:T(8,128)}, u32[]{:S(2)}) copy-start(f32[16,2,1536]{2,0,1:T(8,128)} %get-tuple-element.77) | copy-start | bytes 589828
  277.6 5.0 %copy-start.10 = (f32[16,2,1472]{2,0,1:T(8,128)S(1)}, f32[16,2,1472]{2,0,1:T(8,128)}, u32[]{:S(2)}) copy-start(f32[16,2,1472]{2,0,1:T(8,128)} %slice.760) | copy-start | bytes 565252
  277.6 5.0 %copy-start.11 = (f32[16,2,1472]{2,0,1:T(8,128)S(1)}, f32[16,2,1472]{2,0,1:T(8,128)}, u32[]{:S(2)}) copy-start(f32[16,2,1472]{2,0,1:T(8,128)} %slice.806) | copy-start | bytes 565252
  277.6 5.0 %copy-start.12 = (f32[16,2,1472]{2,0,1:T(8,128)S(1)}, f32[16,2,1472]{2,0,1:T(8,128)}, u32[]{:S(2)}) copy-start(f32[16,2,1472]{2,0,1:T(8,128)} %slice.852) | copy-start | bytes 565252
  277.6 5.0 %copy-start.13 = (f32[16,2,1472]{2,0,1:T(8,128)S(1)}, f32[16,2,1472]{2,0,1:T(8,128)}, u32[]{:S(2)}) copy-start(f32[16,2,1472]{2,0,1:T(8,128)} %slice.750) | copy-start | bytes 565252
  277.6 5.0 %copy-start.14 = (f32[16,2,1472]{2,0,1:T(8,128)S(1)}, f32[16,2,1472]{2,0,1:T(8,128)}, u32[]{:S(2)}) copy-start(f32[16,2,1472]{2,0,1:T(8,128)} %slice.796) | copy-start | bytes 565252
  277.6 5.0 %copy-start.15 = (f32[16,2,1472]{2,0,1:T(8,128)S(1)}, f32[16,2,1472]{2,0,1:T(8,128)}, u32[]{:S(2)}) copy-start(f32[16,2,1472]{2,0,1:T(8,128)} %slice.842) | copy-start | bytes 565252
  277.7 5.0 %copy-start.16 = (f32[16,2,1473]{2,0,1:T(8,128)S(1)}, f32[16,2,1473]{2,0,1:T(8,128)}, u32[]{:S(2)}) copy-start(f32[16,2,1473]{2,0,1:T(8,128)} %slice.735) | copy-start | bytes 565636
  277.7 5.0 %copy-start.17 = (f32[16,2,1535]{2,0,1:T(8,128)S(1)}, f32[16,2,1535]{2,0,1:T(8,128)}, u32[]{:S(2)}) copy-start(f32[16,2,1535]{2,0,1:T(8,128)} %slice.743) | copy-start | bytes 589444
  277.7 5.0 %copy-start.18 = (f32[16,2,1472]{2,0,1:T(8,128)S(1)}, f32[16,2,1472]{2,0,1:T(8,128)}, u32[]{:S(2)}) copy-start(f32[16,2,1472]{2,0,1:T(8,128)} %slice.753) | copy-start | bytes 565252
  277.7 5.0 %copy-start.20 = (f32[16,2,64]{2,0,1:T(8,128)S(1)}, f32[16,2,64]{2,0,1:T(8,128)}, u32[]{:S(2)}) copy-start(f32[16,2,64]{2,0,1:T(8,128)} %slice.761) | copy-start | bytes 24580
  277.7 5.0 %copy-start.21 = (f32[16,2,64]{2,0,1:T(8,128)S(1)}, f32[16,2,64]{2,0,1:T(8,128)}, u32[]{:S(2)}) copy-start(f32[16,2,64]{2,0,1:T(8,128)} %slice.807) | copy-start | bytes 24580
  277.7 5.0 %copy-start.22 = (f32[16,2,64]{2,0,1:T(8,128)S(1)}, f32[16,2,64]{2,0,1:T(8,128)}, u32[]{:S(2)}) copy-start(f32[16,2,64]{2,0,1:T(8,128)} %slice.853) | copy-start | bytes 24580
  277.7 5.0 %copy-start.23 = (f32[16,2,64]{2,0,1:T(8,128)S(1)}, f32[16,2,64]{2,0,1:T(8,128)}, u32[]{:S(2)}) copy-start(f32[16,2,64]{2,0,1:T(8,128)} %slice.751) | copy-start | bytes 24580
  277.7 5.0 %copy-start.24 = (f32[16,2,64]{2,0,1:T(8,128)S(1)}, f32[16,2,64]{2,0,1:T(8,128)}, u32[]{:S(2)}) copy-start(f32[16,2,64]{2,0,1:T(8,128)} %slice.797) | copy-start | bytes 24580
Sparse Core Ops, SparseCore 0:
  25.5 173.7 all-gather.2
  277.7 157.6 reduce-scatter.1
where the time goes:
time: 444 us
  blocking collectives  191 us (43%)
  waiting for transfers between devices  149 us (34%)
  local copies, waits for them, and re-layouts  60.4 us (14%)
  between operations  15.4 us (3%)
  other arithmetic  9.92 us (2%)
  starting transfers between devices  9.55 us (2%)
  matrix products  7.75 us (2%)
    unnamed x1, blocking collectives  191 us
    reduce_scatter x1, waiting for transfers between devices, local(): lax.psum_scatter(filter_local, 'slab', scatter_dimension=2, tiled=True)  149 us
    slice x33, local copies, waits for them, and re-layouts, roll_cells(): values = jnp.roll(values, row_shift * row_width, axis=-1)  17.3 us
  transfers between devices with their start and end apart: 4, of which 2 were waited for; matrix products, arithmetic and copies ran while one was open for 4% of the time, Pallas kernels for 0%

commit v1 on v0

v1 whole, which is shorter than its diff:
```python
import functools
import math

import jax
import jax.numpy as jnp
from jax import lax
from jax.experimental import pallas as pl
from jax.experimental.pallas import tpu as pltpu
from jax.sharding import Mesh, PartitionSpec as P

AXES = ("yl1", "yl0", "x", "core", "yh", "z")
SIZES = (2, 2, 4, 2, 2, 8)
W = 64
PLANE = 1536
BF = jnp.bfloat16
F32 = jnp.float32
SLAB = ("yl1", "yl0", "x", "core")
RING = (0, -1, 1, -2, 2, -3, 3, 4)


def shift_pairs(size, step):
    return [(i, (i + step) % size) for i in range(size)]


def shift_add(rows, sign):
    lane = lax.broadcasted_iota(jnp.int32, (16, 128), 1)
    low = lane < 64
    edge_up = (lane % 64) == 63
    edge_down = (lane % 64) == 0
    count = PLANE // 128
    out = [None] * count
    for r in (-1, 0, 1):
        step = sign * r
        total = []
        taps = []
        for q in (-1, 0, 1):
            v = rows(3 * (q + 1) + r + 1)
            taps.append([v[:, 128 * i : 128 * i + 128] for i in range(count)])
        by_step = {sign * q: taps[q + 1] for q in (-1, 0, 1)}
        up = [pltpu.roll(v, 64, 1) for v in by_step[1]]
        down = [pltpu.roll(v, 64, 1) for v in by_step[-1]]
        for i in range(count):
            a = jnp.where(low, up[i], up[(i + 1) % count])
            b = jnp.where(low, down[(i - 1) % count], down[i])
            total.append(by_step[0][i] + a + b)
        for i in range(count):
            v = total[i]
            if step == 1:
                v = jnp.where(edge_up, pltpu.roll(v, 63, 1), pltpu.roll(v, 127, 1))
            elif step == -1:
                v = jnp.where(edge_down, pltpu.roll(v, 65, 1), pltpu.roll(v, 1, 1))
            out[i] = v if out[i] is None else out[i] + v
    return out


def gather_blocks(z_ref, part, blocks, low, high, field):
    z = z_ref[0]
    for j, off in enumerate(RING):
        row = pl.multiple_of(lax.rem(z + off + 8, 8) * 16, 16)
        for d in range(2):
            field[pl.ds((d + 1) * 128 + row, 16), :] = blocks[j](d)
        field[pl.ds(row, 16), :] = low[part, j]
        field[pl.ds(384 + row, 16), :] = high[part, j]


def conv(field, weights, prod, out_own, out_far, sign):
    for d in range(2):
        prod[...] = jnp.dot(
            weights[...], field[pl.ds(d * 128, 384), :], preferred_element_type=F32
        )
        for m, out in enumerate((out_own, out_far)):
            cols = shift_add(lambda k: prod[pl.ds(m * 144 + k * 16, 16), :], sign)
            for i, v in enumerate(cols):
                out[:, pl.ds(d * PLANE + i * 128, 128)] = v


def blocks_of(refs, last, part):
    def at(j):
        if j == 7:
            return lambda d: last[d]
        return lambda d: refs[j][part, d]

    return [at(j) for j in range(8)]


def features_kernel(z_ref, *refs):
    ring, last, low, high, own, far, weights = refs[:7], *refs[7:13]
    out_own, out_far, out_filter, field, prod, shifted = refs[13:]
    gather_blocks(z_ref, 0, blocks_of(ring, last, 0), low, high, field)
    conv(field, weights, prod, out_own, out_far, 1)
    lane = lax.broadcasted_iota(jnp.int32, (16, 128), 1)
    left = lane < 64
    edge_up = (lane % 64) == 63
    edge_down = (lane % 64) == 0
    count = PLANE // 128
    for m in range(2):
        for d in range(2):
            v = (own[1, d] if m == 0 else far[d]).astype(F32)
            base = [v[:, 128 * i : 128 * i + 128] for i in range(count)]
            for r in (-1, 0, 1):
                if r == 0:
                    col = base
                elif r == 1:
                    col = [jnp.where(edge_down, pltpu.roll(a, 65, 1), pltpu.roll(a, 1, 1)) for a in base]
                else:
                    col = [jnp.where(edge_up, pltpu.roll(a, 63, 1), pltpu.roll(a, 127, 1)) for a in base]
                half = [pltpu.roll(a, 64, 1) for a in col]
                for q in (-1, 0, 1):
                    row = m * 144 + (3 * (q + 1) + r + 1) * 16
                    for i in range(count):
                        if q == 0:
                            a = col[i]
                        elif q == 1:
                            a = jnp.where(left, half[(i - 1) % count], half[i])
                        else:
                            a = jnp.where(left, half[i], half[(i + 1) % count])
                        shifted[pl.ds(row, 16), pl.ds(d * PLANE + i * 128, 128)] = a.astype(BF)
    total = None
    for d in range(2):
        part = lax.dot_general(
            field[pl.ds(d * 128, 384), :],
            shifted[:, pl.ds(d * PLANE, PLANE)],
            (((1,), (1,)), ((), ())),
            preferred_element_type=F32,
        )
        total = part if total is None else total + part
    for m in range(2):
        for p in range(3):
            out_filter[m, :, :, pl.ds(p * 144, 144)] = total[
                p * 128 : p * 128 + 128, m * 144 : m * 144 + 144
            ].reshape(16, 8, 144)


def gradient_kernel(z_ref, *refs):
    ring, last, low, high, weights = refs[:7], *refs[7:11]
    out_own, out_far, field, prod = refs[11:]
    gather_blocks(z_ref, 1, blocks_of(ring, last, 1), low, high, field)
    conv(field, weights, prod, out_own, out_far, -1)


VM = pl.BlockSpec(memory_space=pltpu.VMEM)
SM = pl.BlockSpec(memory_space=pltpu.SMEM)


def local(inputs, filters, cotangent):
    z = lax.axis_index("z")
    yh = lax.axis_index("yh")
    swap = [(0, 1), (1, 0)]
    flat = filters.reshape(432, 256)
    near = lax.dynamic_slice(flat, (0, yh * 128), (432, 128))
    away = lax.dynamic_slice(flat, (0, (1 - yh) * 128), (432, 128))
    far_filters = lax.ppermute(away, "yh", swap)

    row = lax.broadcasted_iota(jnp.int32, (256, 256), 0)
    col = lax.broadcasted_iota(jnp.int32, (256, 256), 1)
    zz, m, i = row // 32, (row // 16) % 2, row % 16
    wanted = ((yh + m) % 2) * 128 + zz * 16 + i
    pick = (col == wanted).astype(BF)
    chunks = lax.dot_general(pick, flat, (((1,), (1,)), ((), ())), preferred_element_type=F32)
    chunks = chunks.astype(BF).reshape(8, 32, 432)
    turned = lax.all_to_all(chunks, "z", 0, 0, tiled=True)
    turned = turned.reshape(8, 2, 16, 3, 9, 16)[:, :, :, ::-1]
    grad_weights = turned.transpose(1, 4, 2, 3, 0, 5).reshape(288, 384)

    def stack_taps(f):
        return f.reshape(3, 144, 128).transpose(1, 0, 2).reshape(144, 384)

    weights = jnp.concatenate([stack_taps(near), stack_taps(far_filters)], 0)

    own = jnp.stack([inputs.transpose(1, 0, 2), cotangent.transpose(1, 0, 2)])
    far = lax.ppermute(own[1], "yh", swap)
    up, down = shift_pairs(8, 1), shift_pairs(8, -1)
    blocks = [own]
    a = b = own
    for _ in range(3):
        a = lax.ppermute(a, "z", up)
        b = lax.ppermute(b, "z", down)
        blocks += [a, b]
    last_x = lax.ppermute(a[0], "z", up)
    last_g = lax.ppermute(b[1], "z", down)

    def rim(d):
        parts = [v[:, d] for v in blocks]
        parts.append(jnp.stack([last_x[d], last_g[d]]))
        return jnp.stack(parts, 1)

    low = lax.ppermute(rim(1), SLAB, shift_pairs(32, 1))
    high = lax.ppermute(rim(0), SLAB, shift_pairs(32, -1))

    zs = z.reshape(1).astype(jnp.int32)
    piece = jax.ShapeDtypeStruct((16, 2 * PLANE), F32)
    params = pltpu.CompilerParams(vmem_limit_bytes=48 * 1024 * 1024)
    feat_own, feat_far, filt = pl.pallas_call(
        features_kernel,
        out_shape=(piece, piece, jax.ShapeDtypeStruct((2, 16, 8, 432), F32)),
        in_specs=[SM] + [VM] * 13,
        out_specs=(VM, VM, VM),
        scratch_shapes=[
            pltpu.VMEM((512, PLANE), BF),
            pltpu.VMEM((288, PLANE), F32),
            pltpu.VMEM((288, 2 * PLANE), BF),
        ],
        compiler_params=params,
    )(zs, *blocks, last_x, low, high, own, far, weights)
    grad_own, grad_far = pl.pallas_call(
        gradient_kernel,
        out_shape=(piece, piece),
        in_specs=[SM] + [VM] * 11,
        out_specs=(VM, VM),
        scratch_shapes=[pltpu.VMEM((512, PLANE), BF), pltpu.VMEM((288, PLANE), F32)],
        compiler_params=params,
    )(zs, *blocks, last_g, low, high, grad_weights)

    feat_in = lax.ppermute(feat_far, "yh", swap)
    grad_in = lax.ppermute(grad_far, "yh", swap)
    got = lax.all_to_all(filt.reshape(32, 8, 432), SLAB, 0, 0, tiled=True)
    factor = 1.0 / math.sqrt(64 * PLANE)
    mine = got.sum(0) * factor
    pairs = []
    for yl1 in range(2):
        for h in range(2):
            pairs.append((yl1 * 2 + h, h * 2 + (yl1 ^ h)))
    mine = lax.ppermute(mine, ("yl1", "yh"), pairs)
    filter_grad = mine.reshape(8, 27, 16).transpose(1, 2, 0)
    features = (feat_own + feat_in).astype(BF).reshape(16, 2, PLANE)
    input_grad = (grad_own + grad_in).astype(BF).reshape(16, 2, PLANE)
    return features, input_grad, filter_grad


def solution(mesh):
    fine = Mesh(mesh.devices.reshape(SIZES), AXES)
    chan = ("yh", "z")
    field = P(chan, SLAB, None)
    return jax.shard_map(
        local,
        mesh=fine,
        in_specs=(field, P(None, chan, None), field),
        out_specs=(field, field, P(None, chan, SLAB)),
        check_vma=False,
    )
```

time: 444 us -> 137 us (0.31)
  the two profiles are of different devices: /device:TPU:64 before, /device:TPU:19 now
where the time goes in v1:
time: 137 us; the launch traced here: 136 us
  starting transfers between devices  74.6 us (54%)
  local copies, waits for them, and re-layouts  33 us (24%)
  waiting for transfers between devices  13.5 us (10%)
  other arithmetic  7.23 us (5%)
  Pallas kernels  5.22 us (4%)
    ppermute x3, starting transfers between devices, local(): b = lax.ppermute(b, 'z', down)  19.9 us
    unnamed x31, local copies, waits for them, and re-layouts  13.1 us
    transpose x2, local copies, waits for them, and re-layouts, local(): grad_weights = turned.transpose(1, 4, 2, 3, 0, 5).reshape(288, 384)  10.6 us
    all_to_all x1, starting transfers between devices, local(): got = lax.all_to_all(filt.reshape(32, 8, 432), SLAB, 0, 0, tiled=True)  9.39 us
    ppermute x1, waiting for transfers between devices, local(): grad_in = lax.ppermute(grad_far, 'yh', swap)  7.83 us
    ppermute x3, starting transfers between devices, local(): a = lax.ppermute(a, 'z', up)  5.76 us
    ppermute x1, starting transfers between devices, local(): high = lax.ppermute(rim(0), SLAB, shift_pairs(32, -1))  5.68 us
    ppermute x1, starting transfers between devices, local(): far_filters = lax.ppermute(away, 'yh', swap)  5.66 us
  transfers between devices with their start and end apart: 17, of which 3 were waited for; matrix products, arithmetic and copies ran while one was open for 25% of the time, Pallas kernels for 2%

profile of v1, /device:TPU:19, one launch (start us, length us, event | category | flops | bytes accessed | tf_op | source)
XLA Modules:
  0.0 135.7 jit_solution(7584863034333271055)
XLA Ops:
  0.6 1.5 %copy.74 = bf16[16,2,1536]{2,0,1:T(8,128)(2,1)} copy(bf16[16,2,1536]{2,1,0:T(2,128)(2,1)} %param.5) | data formatting | bytes 196608 | tf_op args[2]
  2.2 0.9 copy.73
  3.1 0.9 pad_maximum_fusion
  4.0 10.7 %collective-permute-start.1 = (bf16[2,2,16,1536]{3,2,0,1:T(8,128)(2,1)S(1)}, bf16[2,2,16,1536]{3,2,0,1:T(8,128)(2,1)S(1)}, u32[]{:S(2)}, u32[]{:S(2)}) collective-permute-start(bf16[2,2,16,1536]{3,2,0,1:T(8,128)(2,1)S(1)} %pad_maximum_fusion), channel_id=1, source_target_pairs={{0,7},{1,0},{2,1},{3,2},{4,3},{5,4},{6,5},{7,6},{8,15},{9,8},{10,9... | collective-permute-start | bytes 589832 | tf_op jit(solution)/shard_map/ppermute | solution.py:177
  14.7 1.9 %collective-permute-start = (bf16[2,2,16,1536]{3,2,0,1:T(8,128)(2,1)S(1)}, bf16[2,2,16,1536]{3,2,0,1:T(8,128)(2,1)S(1)}, u32[]{:S(2)}, u32[]{:S(2)}) collective-permute-start(bf16[2,2,16,1536]{3,2,0,1:T(8,128)(2,1)S(1)} %pad_maximum_fusion), channel_id=1, source_target_pairs={{0,1},{1,2},{2,3},{3,4},{4,5},{5,6},{6,7},{7,0},{8,9},{9,10},{10,1... | collective-permute-start | bytes 589832 | tf_op jit(solution)/shard_map/ppermute | solution.py:176
  16.6 1.4 %fusion.30 = bf16[2,8,16,1536]{3,2,0,1:T(8,128)(2,1)} fusion(bf16[1,2,16,1536]{3,2,0,1:T(8,128)(2,1)S(1)} %bitcast.79, bf16[1,2,16,1536]{3,2,0,1:T(8,128)(2,1)} %bitcast.68.clone.2), kind=kLoop, calls=%fused_computation.49 | loop fusion | flops 196607 | bytes 294912
  18.1 1.4 %fusion.33 = bf16[2,8,16,1536]{3,2,1,0:T(8,128)(2,1)} fusion(bf16[1,2,16,1536]{3,2,0,1:T(8,128)(2,1)S(1)} %bitcast.80, bf16[1,2,16,1536]{3,2,0,1:T(8,128)(2,1)} %bitcast.68.clone.2), kind=kLoop, calls=%fused_computation.52 | loop fusion | flops 196607 | bytes 294912
  19.5 0.0 collective-permute-done.1
  19.5 4.7 %collective-permute-start.3 = (bf16[2,2,16,1536]{3,2,0,1:T(8,128)(2,1)S(1)}, bf16[2,2,16,1536]{3,2,0,1:T(8,128)(2,1)S(1)}, u32[]{:S(2)}, u32[]{:S(2)}) collective-permute-start(bf16[2,2,16,1536]{3,2,0,1:T(8,128)(2,1)S(1)} %collective-permute-done.1), channel_id=1, source_target_pairs={{0,7},{1,0},{2,1},{3,2},{4,3},{5,4},{6,5},{7,6},{8,15},{9,8},{10,9... | collective-permute-start | bytes 589832 | tf_op jit(solution)/shard_map/ppermute | solution.py:177
  24.2 1.9 %collective-permute-start.2 = (bf16[2,2,16,1536]{3,2,0,1:T(8,128)(2,1)S(1)}, bf16[2,2,16,1536]{3,2,0,1:T(8,128)(2,1)S(1)}, u32[]{:S(2)}, u32[]{:S(2)}) collective-permute-start(bf16[2,2,16,1536]{3,2,0,1:T(8,128)(2,1)S(1)} %collective-permute-done), channel_id=1, source_target_pairs={{0,1},{1,2},{2,3},{3,4},{4,5},{5,6},{6,7},{7,0},{8,9},{9,10},{10,1... | collective-permute-start | bytes 589832 | tf_op jit(solution)/shard_map/ppermute | solution.py:176
  26.2 0.6 slice_dynamic-update-slice_fusion.5
  26.8 0.6 slice_dynamic-update-slice_fusion.4
  27.5 0.7 fusion.39
  28.1 0.6 fusion.38
  28.7 0.0 collective-permute-done.3
  28.7 4.6 %collective-permute-start.5 = (bf16[2,2,16,1536]{3,2,0,1:T(8,128)(2,1)S(1)}, bf16[2,2,16,1536]{3,2,0,1:T(8,128)(2,1)S(1)}, u32[]{:S(2)}, u32[]{:S(2)}) collective-permute-start(bf16[2,2,16,1536]{3,2,0,1:T(8,128)(2,1)S(1)} %collective-permute-done.3), channel_id=1, source_target_pairs={{0,7},{1,0},{2,1},{3,2},{4,3},{5,4},{6,5},{7,6},{8,15},{9,8},{10,9... | collective-permute-start | bytes 589832 | tf_op jit(solution)/shard_map/ppermute | solution.py:177
  33.3 0.0 collective-permute-done.2
  33.3 1.9 %collective-permute-start.4 = (bf16[2,2,16,1536]{3,2,0,1:T(8,128)(2,1)S(1)}, bf16[2,2,16,1536]{3,2,0,1:T(8,128)(2,1)S(1)}, u32[]{:S(2)}, u32[]{:S(2)}) collective-permute-start(bf16[2,2,16,1536]{3,2,0,1:T(8,128)(2,1)S(1)} %collective-permute-done.2), channel_id=1, source_target_pairs={{0,1},{1,2},{2,3},{3,4},{4,5},{5,6},{6,7},{7,0},{8,9},{9,10},{10,1... | collective-permute-start | bytes 589832 | tf_op jit(solution)/shard_map/ppermute | solution.py:176
  35.3 0.7 slice_dynamic-update-slice_fusion.3
  35.9 0.6 slice_dynamic-update-slice_fusion.2
  36.6 0.6 fusion.37
  37.2 0.7 fusion.36
  37.9 0.0 collective-permute-done.5
  37.9 4.6 %collective-permute-start.7 = (bf16[2,16,1536]{2,1,0:T(8,128)(2,1)S(1)}, bf16[2,16,1536]{2,1,0:T(8,128)(2,1)S(1)}, u32[]{:S(2)}, u32[]{:S(2)}) collective-permute-start(bf16[2,16,1536]{2,1,0:T(8,128)(2,1)S(1)} %slice_bitcast_fusion.6), channel_id=1, source_target_pairs={{0,7},{1,0},{2,1},{3,2},{4,3},{5,4},{6,5},{7,6},{8,15},{9,8},{10,9... | collective-permute-start | bytes 294920 | tf_op jit(solution)/shard_map/ppermute | solution.py:180
  42.5 0.0 collective-permute-done.4
  42.5 1.9 %collective-permute-start.6 = (bf16[2,16,1536]{2,1,0:T(8,128)(2,1)S(1)}, bf16[2,16,1536]{2,1,0:T(8,128)(2,1)S(1)}, u32[]{:S(2)}, u32[]{:S(2)}) collective-permute-start(bf16[2,16,1536]{2,1,0:T(8,128)(2,1)S(1)} %slice_bitcast_fusion.7), channel_id=1, source_target_pairs={{0,1},{1,2},{2,3},{3,4},{4,5},{5,6},{6,7},{7,0},{8,9},{9,10},{10,1... | collective-permute-start | bytes 294920 | tf_op jit(solution)/shard_map/ppermute | solution.py:179
  44.4 0.6 slice_dynamic-update-slice_fusion.1
  45.0 0.6 slice_dynamic-update-slice_fusion
  45.7 0.6 fusion.35
  46.3 0.7 fusion.34
  47.0 2.1 %collective-permute-done.6.refs_7_ = bf16[2,16,1536]{2,1,0:T(8,128)(2,1)S(1)} collective-permute-done((bf16[2,16,1536]{2,1,0:T(8,128)(2,1)S(1)}, bf16[2,16,1536]{2,1,0:T(8,128)(2,1)S(1)}, u32[]{:S(2)}, u32[]{:S(2)}) %collective-permute-start.6) | collective-permute-done | bytes 98336 | tf_op jit(solution)/shard_map/ppermute | solution.py:179
  49.1 0.7 fusion.41
  49.7 5.7 %collective-permute-start.9 = (bf16[2,8,16,1536]{3,2,1,0:T(8,128)(2,1)}, bf16[2,8,16,1536]{3,2,1,0:T(8,128)(2,1)S(1)}, u32[]{:S(2)}, u32[]{:S(2)}) collective-permute-start(bf16[2,8,16,1536]{3,2,1,0:T(8,128)(2,1)} %fusion.41), channel_id=1, source_target_pairs={{0,496},{16,0},{32,16},{48,32},{64,48},{80,64},{96,80},{112,96},{1... | collective-permute-start | bytes 2359304 | tf_op jit(solution)/shard_map/ppermute | solution.py:188
  55.4 0.6 fusion.40
  56.1 3.0 %collective-permute-start.8 = (bf16[2,8,16,1536]{3,2,0,1:T(8,128)(2,1)}, bf16[2,8,16,1536]{3,2,0,1:T(8,128)(2,1)}, u32[]{:S(2)}, u32[]{:S(2)}) collective-permute-start(bf16[2,8,16,1536]{3,2,0,1:T(8,128)(2,1)} %fusion.40), channel_id=1, source_target_pairs={{0,16},{16,32},{32,48},{48,64},{64,80},{80,96},{96,112},{112,128},... | collective-permute-start | bytes 2359304 | tf_op jit(solution)/shard_map/ppermute | solution.py:187
  59.1 1.0 convolution_convert_fusion
  60.2 0.8 copy.52
  61.0 3.4 %all-to-all-start = ((bf16[8,32,432]{2,1,0:T(8,128)(2,1)}), bf16[8,32,432]{2,1,0:T(8,128)(2,1)S(1)}, u32[]{:S(2)}, u32[]{:S(2)}) async-start(bf16[8,32,432]{2,1,0:T(8,128)(2,1)} %bitcast.21), calls=%async_computation | async-start | bytes 524288 | tf_op jit(solution)/shard_map/all_to_all | solution.py:161
  64.5 5.7 %collective-permute-start.11 = (bf16[432,128]{1,0:T(8,128)(2,1)S(1)}, bf16[432,128]{1,0:T(8,128)(2,1)S(1)}, u32[]{:S(2)}, u32[]{:S(2)}) collective-permute-start(bf16[432,128]{1,0:T(8,128)(2,1)S(1)} %get-tuple-element.17), channel_id=1, source_target_pairs={{0,8},{8,0},{1,9},{9,1},{2,10},{10,2},{3,11},{11,3},{4,12},{12,4},... | collective-permute-start | bytes 331784 | tf_op jit(solution)/shard_map/ppermute | solution.py:152
  70.1 3.5 %collective-permute-start.10 = (bf16[2,16,1536]{2,1,0:T(8,128)(2,1)}, bf16[2,16,1536]{2,1,0:T(8,128)(2,1)S(1)}, u32[]{:S(2)}, u32[]{:S(2)}) collective-permute-start(bf16[2,16,1536]{2,1,0:T(8,128)(2,1)} %bitcast.76), channel_id=1, source_target_pairs={{0,8},{8,0},{1,9},{9,1},{2,10},{10,2},{3,11},{11,3},{4,12},{12,4},... | collective-permute-start | bytes 294920 | tf_op jit(solution)/shard_map/ppermute | solution.py:171
  73.7 3.6 %collective-permute-done.11 = bf16[432,128]{1,0:T(8,128)(2,1)S(1)} collective-permute-done((bf16[432,128]{1,0:T(8,128)(2,1)S(1)}, bf16[432,128]{1,0:T(8,128)(2,1)S(1)}, u32[]{:S(2)}, u32[]{:S(2)}) %collective-permute-start.11) | collective-permute-done | bytes 110624 | tf_op jit(solution)/shard_map/ppermute | solution.py:152
  77.5 0.4 copy.53
  77.9 1.7 %reshape.53 = bf16[8,2,16,3,9,16]{2,1,5,4,3,0:T(2,128)(2,1)} reshape(bf16[8,32,432]{1,2,0:T(8,128)(2,1)S(1)} %copy.53) | data formatting | bytes 442368 | tf_op jit(solution)/shard_map/reshape | solution.py:162
  79.6 0.9 copy.46.refs_3_
  80.6 1.2 copy.50.refs_8_
  81.8 3.0 %shard_map.58 = (f32[16,3072]{1,0:T(8,128)S(1)}, f32[16,3072]{1,0:T(8,128)S(1)}, f32[2,16,8,432]{3,2,1,0:T(8,128)S(1)}) custom-call(s32[1]{0:T(128)} %bitcast.z_ref, bf16[2,2,16,1536]{3,2,1,0:T(8,128)(2,1)S(1)} %copy.43.refs_0_.refs_10_, bf16[2,2,16,1536]{3,2,1,0:T(8,128)(2,1)S(1)} %copy.44.refs_1_, bf16[2,2,16,1536]{3,2,1,0:T(8,128)(2,1)S(1)} %copy.45.refs_2_, ...), custom_call_target="tpu_custom_call" | custom-call | tf_op jit(solution)/shard_map/pallas_call | solution.py:193
  84.8 0.8 copy-done
  85.6 0.7 copy-done.1
  86.3 0.7 copy-done.3
  87.0 9.4 %all-to-all-start.1 = ((f32[32,8,432]{2,1,0:T(8,128)}), f32[32,8,432]{2,1,0:T(8,128)}, u32[]{:S(2)}, u32[]{:S(2)}) async-start(f32[32,8,432]{2,1,0:T(8,128)} %bitcast.77), calls=%async_computation.1 | async-start | bytes 1048576 | tf_op jit(solution)/shard_map/all_to_all | solution.py:216
  96.4 4.4 %collective-permute-start.12 = (f32[16,3072]{1,0:T(8,128)}, f32[16,3072]{1,0:T(8,128)}, u32[]{:S(2)}, u32[]{:S(2)}) collective-permute-start(f32[16,3072]{1,0:T(8,128)} %copy-done.3), channel_id=1, source_target_pairs={{0,8},{8,0},{1,9},{9,1},{2,10},{10,2},{3,11},{11,3},{4,12},{12,4},... | collective-permute-start | bytes 589832 | tf_op jit(solution)/shard_map/ppermute | solution.py:214
  100.8 3.9 %reverse_bitcast_fusion = bf16[2,9,16,3,8,16]{2,0,5,1,3,4:T(2,128)(2,1)} fusion(bf16[8,2,16,3,9,16]{2,1,5,4,3,0:T(2,128)(2,1)} %reshape.53), kind=kLoop, calls=%fused_computation | loop fusion | bytes 442368 | tf_op jit(solution)/shard_map/transpose | solution.py:163
  104.7 6.7 %copy.54 = bf16[2,9,16,3,8,16]{5,4,3,2,1,0:T(8,128)(2,1)} copy(bf16[2,9,16,3,8,16]{2,0,5,1,3,4:T(2,128)(2,1)} %reverse_bitcast_fusion) | data formatting | bytes 442368 | tf_op jit(solution)/shard_map/transpose | solution.py:163
  111.4 2.5 %reshape.54.refs_10_ = bf16[288,384]{1,0:T(8,128)(2,1)S(1)} reshape(bf16[2,9,16,3,8,16]{5,4,3,2,1,0:T(8,128)(2,1)} %copy.54) | data formatting | bytes 442368 | tf_op jit(solution)/shard_map/reshape | solution.py:163
  114.0 2.2 %shard_map.59 = (f32[16,3072]{1,0:T(8,128)S(1)}, f32[16,3072]{1,0:T(8,128)}) custom-call(s32[1]{0:T(128)} %bitcast.z_ref, bf16[2,2,16,1536]{3,2,1,0:T(8,128)(2,1)S(1)} %copy.43.refs_0_.refs_10_, bf16[2,2,16,1536]{3,2,1,0:T(8,128)(2,1)S(1)} %copy.44.refs_1_, bf16[2,2,16,1536]{3,2,1,0:T(8,128)(2,1)S(1)} %copy.45.refs_2_, ...), custom_call_target="tpu_custom_call" | custom-call | tf_op jit(solution)/shard_map/pallas_call | solution.py:205
  116.2 4.8 %collective-permute-start.13 = (f32[16,3072]{1,0:T(8,128)}, f32[16,3072]{1,0:T(8,128)S(1)}, u32[]{:S(2)}, u32[]{:S(2)}) collective-permute-start(f32[16,3072]{1,0:T(8,128)} %get-tuple-element.11), channel_id=1, source_target_pairs={{0,8},{8,0},{1,9},{9,1},{2,10},{10,2},{3,11},{11,3},{4,12},{12,4},... | collective-permute-start | bytes 589832 | tf_op jit(solution)/shard_map/ppermute | solution.py:215
  121.0 1.0 add_convert_fusion.1
  121.9 1.1 reduce_sum.9
  123.0 2.6 %collective-permute-start.14 = (f32[8,432]{1,0:T(8,128)S(1)}, f32[8,432]{1,0:T(8,128)S(1)}, u32[]{:S(2)}, u32[]{:S(2)}) collective-permute-start(f32[8,432]{1,0:T(8,128)S(1)} %broadcast_multiply_fusion), channel_id=1, source_target_pairs={{0,0},{8,264},{256,8},{264,256},{1,1},{9,265},{257,9},{265,257},{2... | collective-permute-start | bytes 41480 | tf_op jit(solution)/shard_map/ppermute | solution.py:223
  125.7 7.8 %collective-permute-done.13 = f32[16,3072]{1,0:T(8,128)S(1)} collective-permute-done((f32[16,3072]{1,0:T(8,128)}, f32[16,3072]{1,0:T(8,128)S(1)}, u32[]{:S(2)}, u32[]{:S(2)}) %collective-permute-start.13) | collective-permute-done | bytes 196640 | tf_op jit(solution)/shard_map/ppermute | solution.py:215
  133.5 0.7 reshape.51
  134.2 0.7 reshape.55
  134.9 0.1 reshape.57
  135.0 0.7 copy.63
  (43 shorter events, 0.3 us)
Async XLA Ops:
  4.0 15.5 %collective-permute-start.1 = (bf16[2,2,16,1536]{3,2,0,1:T(8,128)(2,1)S(1)}, bf16[2,2,16,1536]{3,2,0,1:T(8,128)(2,1)S(1)}, u32[]{:S(2)}, u32[]{:S(2)}) collective-permute-start(bf16[2,2,16,1536]{3,2,0,1:T(8,128)(2,1)S(1)} %pad_maximum_fusion), channel_id=1, source_target_pairs={{0,7},{1,0},{2,1},{3,2},{4,3},{5,4},{6,5},{7,6},{8,15},{9,8},{10,9... | collective-permute-start | bytes 589832 | tf_op jit(solution)/shard_map/ppermute | solution.py:177
  14.7 9.6 %collective-permute-start = (bf16[2,2,16,1536]{3,2,0,1:T(8,128)(2,1)S(1)}, bf16[2,2,16,1536]{3,2,0,1:T(8,128)(2,1)S(1)}, u32[]{:S(2)}, u32[]{:S(2)}) collective-permute-start(bf16[2,2,16,1536]{3,2,0,1:T(8,128)(2,1)S(1)} %pad_maximum_fusion), channel_id=1, source_target_pairs={{0,1},{1,2},{2,3},{3,4},{4,5},{5,6},{6,7},{7,0},{8,9},{9,10},{10,1... | collective-permute-start | bytes 589832 | tf_op jit(solution)/shard_map/ppermute | solution.py:176
  19.5 39.6 %copy-start.7 = (bf16[27,16,256]{2,1,0:T(8,128)(2,1)S(1)}, bf16[27,16,256]{2,1,0:T(8,128)(2,1)}, u32[]{:S(2)}) copy-start(bf16[27,16,256]{2,1,0:T(8,128)(2,1)} %param.4) | copy-start | bytes 663556
  19.5 9.2 %collective-permute-start.3 = (bf16[2,2,16,1536]{3,2,0,1:T(8,128)(2,1)S(1)}, bf16[2,2,16,1536]{3,2,0,1:T(8,128)(2,1)S(1)}, u32[]{:S(2)}, u32[]{:S(2)}) collective-permute-start(bf16[2,2,16,1536]{3,2,0,1:T(8,128)(2,1)S(1)} %collective-permute-done.1), channel_id=1, source_target_pairs={{0,7},{1,0},{2,1},{3,2},{4,3},{5,4},{6,5},{7,6},{8,15},{9,8},{10,9... | collective-permute-start | bytes 589832 | tf_op jit(solution)/shard_map/ppermute | solution.py:177
  24.2 9.1 %collective-permute-start.2 = (bf16[2,2,16,1536]{3,2,0,1:T(8,128)(2,1)S(1)}, bf16[2,2,16,1536]{3,2,0,1:T(8,128)(2,1)S(1)}, u32[]{:S(2)}, u32[]{:S(2)}) collective-permute-start(bf16[2,2,16,1536]{3,2,0,1:T(8,128)(2,1)S(1)} %collective-permute-done), channel_id=1, source_target_pairs={{0,1},{1,2},{2,3},{3,4},{4,5},{5,6},{6,7},{7,0},{8,9},{9,10},{10,1... | collective-permute-start | bytes 589832 | tf_op jit(solution)/shard_map/ppermute | solution.py:176
  28.7 31.4 %copy-start.4 = (bf16[2,2,16,1536]{3,2,0,1:T(8,128)(2,1)}, bf16[2,2,16,1536]{3,2,0,1:T(8,128)(2,1)S(1)}, u32[]{:S(2)}) copy-start(bf16[2,2,16,1536]{3,2,0,1:T(8,128)(2,1)S(1)} %collective-permute-done.3) | copy-start | bytes 589828
  28.7 9.1 %collective-permute-start.5 = (bf16[2,2,16,1536]{3,2,0,1:T(8,128)(2,1)S(1)}, bf16[2,2,16,1536]{3,2,0,1:T(8,128)(2,1)S(1)}, u32[]{:S(2)}, u32[]{:S(2)}) collective-permute-start(bf16[2,2,16,1536]{3,2,0,1:T(8,128)(2,1)S(1)} %collective-permute-done.3), channel_id=1, source_target_pairs={{0,7},{1,0},{2,1},{3,2},{4,3},{5,4},{6,5},{7,6},{8,15},{9,8},{10,9... | collective-permute-start | bytes 589832 | tf_op jit(solution)/shard_map/ppermute | solution.py:177
  33.3 26.8 %copy-start.6 = (bf16[2,2,16,1536]{3,2,0,1:T(8,128)(2,1)}, bf16[2,2,16,1536]{3,2,0,1:T(8,128)(2,1)S(1)}, u32[]{:S(2)}) copy-start(bf16[2,2,16,1536]{3,2,0,1:T(8,128)(2,1)S(1)} %collective-permute-done.2) | copy-start | bytes 589828
  33.3 9.1 %collective-permute-start.4 = (bf16[2,2,16,1536]{3,2,0,1:T(8,128)(2,1)S(1)}, bf16[2,2,16,1536]{3,2,0,1:T(8,128)(2,1)S(1)}, u32[]{:S(2)}, u32[]{:S(2)}) collective-permute-start(bf16[2,2,16,1536]{3,2,0,1:T(8,128)(2,1)S(1)} %collective-permute-done.2), channel_id=1, source_target_pairs={{0,1},{1,2},{2,3},{3,4},{4,5},{5,6},{6,7},{7,0},{8,9},{9,10},{10,1... | collective-permute-start | bytes 589832 | tf_op jit(solution)/shard_map/ppermute | solution.py:176
  37.9 9.1 %collective-permute-start.7 = (bf16[2,16,1536]{2,1,0:T(8,128)(2,1)S(1)}, bf16[2,16,1536]{2,1,0:T(8,128)(2,1)S(1)}, u32[]{:S(2)}, u32[]{:S(2)}) collective-permute-start(bf16[2,16,1536]{2,1,0:T(8,128)(2,1)S(1)} %slice_bitcast_fusion.6), channel_id=1, source_target_pairs={{0,7},{1,0},{2,1},{3,2},{4,3},{5,4},{6,5},{7,6},{8,15},{9,8},{10,9... | collective-permute-start | bytes 294920 | tf_op jit(solution)/shard_map/ppermute | solution.py:180
  42.5 6.6 %collective-permute-start.6 = (bf16[2,16,1536]{2,1,0:T(8,128)(2,1)S(1)}, bf16[2,16,1536]{2,1,0:T(8,128)(2,1)S(1)}, u32[]{:S(2)}, u32[]{:S(2)}) collective-permute-start(bf16[2,16,1536]{2,1,0:T(8,128)(2,1)S(1)} %slice_bitcast_fusion.7), channel_id=1, source_target_pairs={{0,1},{1,2},{2,3},{3,4},{4,5},{5,6},{6,7},{7,0},{8,9},{9,10},{10,1... | collective-permute-start | bytes 294920 | tf_op jit(solution)/shard_map/ppermute | solution.py:179
  49.7 32.1 %collective-permute-start.9 = (bf16[2,8,16,1536]{3,2,1,0:T(8,128)(2,1)}, bf16[2,8,16,1536]{3,2,1,0:T(8,128)(2,1)S(1)}, u32[]{:S(2)}, u32[]{:S(2)}) collective-permute-start(bf16[2,8,16,1536]{3,2,1,0:T(8,128)(2,1)} %fusion.41), channel_id=1, source_target_pairs={{0,496},{16,0},{32,16},{48,32},{64,48},{80,64},{96,80},{112,96},{1... | collective-permute-start | bytes 2359304 | tf_op jit(solution)/shard_map/ppermute | solution.py:188
  56.1 24.6 %collective-permute-start.8 = (bf16[2,8,16,1536]{3,2,0,1:T(8,128)(2,1)}, bf16[2,8,16,1536]{3,2,0,1:T(8,128)(2,1)}, u32[]{:S(2)}, u32[]{:S(2)}) collective-permute-start(bf16[2,8,16,1536]{3,2,0,1:T(8,128)(2,1)} %fusion.40), channel_id=1, source_target_pairs={{0,16},{16,32},{32,48},{48,64},{64,80},{80,96},{96,112},{112,128},... | collective-permute-start | bytes 2359304 | tf_op jit(solution)/shard_map/ppermute | solution.py:187
  61.0 16.4 %all-to-all-start = ((bf16[8,32,432]{2,1,0:T(8,128)(2,1)}), bf16[8,32,432]{2,1,0:T(8,128)(2,1)S(1)}, u32[]{:S(2)}, u32[]{:S(2)}) async-start(bf16[8,32,432]{2,1,0:T(8,128)(2,1)} %bitcast.21), calls=%async_computation | async-start | bytes 524288 | tf_op jit(solution)/shard_map/all_to_all | solution.py:161
  64.5 12.9 %collective-permute-start.11 = (bf16[432,128]{1,0:T(8,128)(2,1)S(1)}, bf16[432,128]{1,0:T(8,128)(2,1)S(1)}, u32[]{:S(2)}, u32[]{:S(2)}) collective-permute-start(bf16[432,128]{1,0:T(8,128)(2,1)S(1)} %get-tuple-element.17), channel_id=1, source_target_pairs={{0,8},{8,0},{1,9},{9,1},{2,10},{10,2},{3,11},{11,3},{4,12},{12,4},... | collective-permute-start | bytes 331784 | tf_op jit(solution)/shard_map/ppermute | solution.py:152
  70.1 11.7 %collective-permute-start.10 = (bf16[2,16,1536]{2,1,0:T(8,128)(2,1)}, bf16[2,16,1536]{2,1,0:T(8,128)(2,1)S(1)}, u32[]{:S(2)}, u32[]{:S(2)}) collective-permute-start(bf16[2,16,1536]{2,1,0:T(8,128)(2,1)} %bitcast.76), channel_id=1, source_target_pairs={{0,8},{8,0},{1,9},{9,1},{2,10},{10,2},{3,11},{11,3},{4,12},{12,4},... | collective-permute-start | bytes 294920 | tf_op jit(solution)/shard_map/ppermute | solution.py:171
  77.9 1.7 %copy-start.5 = (bf16[2,2,16,1536]{3,2,0,1:T(8,128)(2,1)S(1)}, bf16[2,2,16,1536]{3,2,0,1:T(8,128)(2,1)}, u32[]{:S(2)}) copy-start(bf16[2,2,16,1536]{3,2,0,1:T(8,128)(2,1)} %copy-done.4) | copy-start | bytes 589828
  84.8 0.8 copy-start
  85.6 0.7 copy-start.1
  86.3 0.7 copy-start.3
  87.0 34.9 %all-to-all-start.1 = ((f32[32,8,432]{2,1,0:T(8,128)}), f32[32,8,432]{2,1,0:T(8,128)}, u32[]{:S(2)}, u32[]{:S(2)}) async-start(f32[32,8,432]{2,1,0:T(8,128)} %bitcast.77), calls=%async_computation.1 | async-start | bytes 1048576 | tf_op jit(solution)/shard_map/all_to_all | solution.py:216
  96.4 24.6 %collective-permute-start.12 = (f32[16,3072]{1,0:T(8,128)}, f32[16,3072]{1,0:T(8,128)}, u32[]{:S(2)}, u32[]{:S(2)}) collective-permute-start(f32[16,3072]{1,0:T(8,128)} %copy-done.3), channel_id=1, source_target_pairs={{0,8},{8,0},{1,9},{9,1},{2,10},{10,2},{3,11},{11,3},{4,12},{12,4},... | collective-permute-start | bytes 589832 | tf_op jit(solution)/shard_map/ppermute | solution.py:214
  114.0 7.0 %copy-start.2 = (f32[16,3072]{1,0:T(8,128)S(1)}, f32[16,3072]{1,0:T(8,128)}, u32[]{:S(2)}) copy-start(f32[16,3072]{1,0:T(8,128)} %copy-done.1) | copy-start | bytes 589828
  116.2 17.3 %collective-permute-start.13 = (f32[16,3072]{1,0:T(8,128)}, f32[16,3072]{1,0:T(8,128)S(1)}, u32[]{:S(2)}, u32[]{:S(2)}) collective-permute-start(f32[16,3072]{1,0:T(8,128)} %get-tuple-element.11), channel_id=1, source_target_pairs={{0,8},{8,0},{1,9},{9,1},{2,10},{10,2},{3,11},{11,3},{4,12},{12,4},... | collective-permute-start | bytes 589832 | tf_op jit(solution)/shard_map/ppermute | solution.py:215
  123.0 11.9 %collective-permute-start.14 = (f32[8,432]{1,0:T(8,128)S(1)}, f32[8,432]{1,0:T(8,128)S(1)}, u32[]{:S(2)}, u32[]{:S(2)}) collective-permute-start(f32[8,432]{1,0:T(8,128)S(1)} %broadcast_multiply_fusion), channel_id=1, source_target_pairs={{0,0},{8,264},{256,8},{264,256},{1,1},{9,265},{257,9},{265,257},{2... | collective-permute-start | bytes 41480 | tf_op jit(solution)/shard_map/ppermute | solution.py:223

commit v2 on v1

--- a/solution.py
+++ b/solution.py
@@ -53,14 +53,15 @@
     return out
 
 
-def gather_blocks(z_ref, part, blocks, low, high, field):
-    z = z_ref[0]
+def gather_blocks(info, part, blocks, inner, outer, field):
+    z, core = info[0], info[1]
+    inner_at, outer_at = (1 - core) * 384, core * 384
     for j, off in enumerate(RING):
         row = pl.multiple_of(lax.rem(z + off + 8, 8) * 16, 16)
         for d in range(2):
             field[pl.ds((d + 1) * 128 + row, 16), :] = blocks[j](d)
-        field[pl.ds(row, 16), :] = low[part, j]
-        field[pl.ds(384 + row, 16), :] = high[part, j]
+        field[pl.ds(pl.multiple_of(inner_at + row, 16), 16), :] = inner[j, part]
+        field[pl.ds(pl.multiple_of(outer_at + row, 16), 16), :] = outer[j, part]
 
 
 def conv(field, weights, prod, out_own, out_far, sign):
@@ -78,16 +79,77 @@
     def at(j):
         if j == 7:
             return lambda d: last[d]
-        return lambda d: refs[j][part, d]
+        return lambda d: refs[j][d, part]
 
     return [at(j) for j in range(8)]
 
 
-def features_kernel(z_ref, *refs):
-    ring, last, low, high, own, far, weights = refs[:7], *refs[7:13]
-    out_own, out_far, out_filter, field, prod, shifted = refs[13:]
-    gather_blocks(z_ref, 0, blocks_of(ring, last, 0), low, high, field)
+def grad_weights(turned, weights):
+    lane = lax.broadcasted_iota(jnp.int32, (32, 128), 1) // 16
+    got = [turned[k].astype(F32) for k in range(8)]
+    for t in range(27):
+        p, qr = t // 9, t % 9
+        lo = t * 16 // 128 * 128
+        total = None
+        for k in range(8):
+            v = got[k][:, lo : lo + 128]
+            v = pltpu.roll(v, (16 * k - (t * 16 - lo)) % 128, 1)
+            total = v if total is None else jnp.where(lane == k, v, total)
+        total = total.astype(BF)
+        for m in range(2):
+            weights[pl.ds(m * 144 + qr * 16, 16), pl.ds((2 - p) * 128, 128)] = total[
+                16 * m : 16 * m + 16
+            ]
+
+
+def rims_kernel(info, *refs):
+    ring, last_x, last_g = refs[:7], *refs[7:9]
+    inner, outer = refs[9:]
+    core = info[1]
+    for j in range(7):
+        inner[j] = ring[j][1 - core]
+        outer[j] = ring[j][core]
+    inner[7, 0] = last_x[1 - core]
+    inner[7, 1] = last_g[1 - core]
+    outer[7, 0] = last_x[core]
+    outer[7, 1] = last_g[core]
+
+
+def features_kernel(info, *refs):
+    ring, last, inner, outer, near, away = refs[:7], *refs[7:12]
+    out_own, out_far, field, prod, weights = refs[12:]
+    gather_blocks(info, 0, blocks_of(ring, last, 0), inner, outer, field)
+    for m, f in enumerate((near, away)):
+        for p in range(3):
+            weights[pl.ds(m * 144, 144), pl.ds(p * 128, 128)] = f[pl.ds(p * 144, 144), :]
     conv(field, weights, prod, out_own, out_far, 1)
+
+
+def filter_kernel(info, *refs):
+    ring, last, inner, outer, far, _after = refs[:7], *refs[7:12]
+    out_filter, field, shifted = refs[12:]
+    gather_blocks(info, 0, blocks_of(ring, last, 0), inner, outer, field)
+    filter_part(ring[0], far, field, shifted, out_filter)
+
+
+def gradient_kernel(info, *refs):
+    ring, last, inner, outer, turned, _after = refs[:7], *refs[7:12]
+    out_own, out_far, field, prod, weights = refs[12:]
+    gather_blocks(info, 1, blocks_of(ring, last, 1), inner, outer, field)
+    grad_weights(turned, weights)
+    conv(field, weights, prod, out_own, out_far, -1)
+
+
+def chunks_kernel(pick, flat, _after, out):
+    v = lax.dot_general(
+        pick[...], flat[...], (((1,), (1,)), ((), ())), preferred_element_type=F32
+    ).astype(BF)
+    for k in range(8):
+        out[k, :, pl.ds(0, 432)] = v[32 * k : 32 * k + 32]
+        out[k, :, pl.ds(432, 80)] = jnp.zeros((32, 80), BF)
+
+
+def filter_part(own, far, x_field, shifted, out_filter):
     lane = lax.broadcasted_iota(jnp.int32, (16, 128), 1)
     left = lane < 64
     edge_up = (lane % 64) == 63
@@ -95,7 +157,7 @@
     count = PLANE // 128
     for m in range(2):
         for d in range(2):
-            v = (own[1, d] if m == 0 else far[d]).astype(F32)
+            v = (own[d, 1] if m == 0 else far[d]).astype(F32)
             base = [v[:, 128 * i : 128 * i + 128] for i in range(count)]
             for r in (-1, 0, 1):
                 if r == 0:
@@ -118,7 +180,7 @@
     total = None
     for d in range(2):
         part = lax.dot_general(
-            field[pl.ds(d * 128, 384), :],
+            x_field[pl.ds(d * 128, 384), :],
             shifted[:, pl.ds(d * PLANE, PLANE)],
             (((1,), (1,)), ((), ())),
             preferred_element_type=F32,
@@ -131,15 +193,9 @@
             ].reshape(16, 8, 144)
 
 
-def gradient_kernel(z_ref, *refs):
-    ring, last, low, high, weights = refs[:7], *refs[7:11]
-    out_own, out_far, field, prod = refs[11:]
-    gather_blocks(z_ref, 1, blocks_of(ring, last, 1), low, high, field)
-    conv(field, weights, prod, out_own, out_far, -1)
-
-
 VM = pl.BlockSpec(memory_space=pltpu.VMEM)
 SM = pl.BlockSpec(memory_space=pltpu.SMEM)
+ANY = pl.BlockSpec(memory_space=pl.ANY)
 
 
 def local(inputs, filters, cotangent):
@@ -156,19 +212,8 @@
     zz, m, i = row // 32, (row // 16) % 2, row % 16
     wanted = ((yh + m) % 2) * 128 + zz * 16 + i
     pick = (col == wanted).astype(BF)
-    chunks = lax.dot_general(pick, flat, (((1,), (1,)), ((), ())), preferred_element_type=F32)
-    chunks = chunks.astype(BF).reshape(8, 32, 432)
-    turned = lax.all_to_all(chunks, "z", 0, 0, tiled=True)
-    turned = turned.reshape(8, 2, 16, 3, 9, 16)[:, :, :, ::-1]
-    grad_weights = turned.transpose(1, 4, 2, 3, 0, 5).reshape(288, 384)
-
-    def stack_taps(f):
-        return f.reshape(3, 144, 128).transpose(1, 0, 2).reshape(144, 384)
-
-    weights = jnp.concatenate([stack_taps(near), stack_taps(far_filters)], 0)
-
-    own = jnp.stack([inputs.transpose(1, 0, 2), cotangent.transpose(1, 0, 2)])
-    far = lax.ppermute(own[1], "yh", swap)
+    own = jnp.stack([inputs, cotangent]).transpose(2, 0, 1, 3)
+    far = lax.ppermute(own[:, 1], "yh", swap)
     up, down = shift_pairs(8, 1), shift_pairs(8, -1)
     blocks = [own]
     a = b = own
@@ -176,44 +221,48 @@
         a = lax.ppermute(a, "z", up)
         b = lax.ppermute(b, "z", down)
         blocks += [a, b]
-    last_x = lax.ppermute(a[0], "z", up)
-    last_g = lax.ppermute(b[1], "z", down)
-
-    def rim(d):
-        parts = [v[:, d] for v in blocks]
-        parts.append(jnp.stack([last_x[d], last_g[d]]))
-        return jnp.stack(parts, 1)
-
-    low = lax.ppermute(rim(1), SLAB, shift_pairs(32, 1))
-    high = lax.ppermute(rim(0), SLAB, shift_pairs(32, -1))
-
-    zs = z.reshape(1).astype(jnp.int32)
-    piece = jax.ShapeDtypeStruct((16, 2 * PLANE), F32)
-    params = pltpu.CompilerParams(vmem_limit_bytes=48 * 1024 * 1024)
-    feat_own, feat_far, filt = pl.pallas_call(
-        features_kernel,
-        out_shape=(piece, piece, jax.ShapeDtypeStruct((2, 16, 8, 432), F32)),
-        in_specs=[SM] + [VM] * 13,
-        out_specs=(VM, VM, VM),
-        scratch_shapes=[
-            pltpu.VMEM((512, PLANE), BF),
-            pltpu.VMEM((288, PLANE), F32),
-            pltpu.VMEM((288, 2 * PLANE), BF),
-        ],
-        compiler_params=params,
-    )(zs, *blocks, last_x, low, high, own, far, weights)
-    grad_own, grad_far = pl.pallas_call(
-        gradient_kernel,
-        out_shape=(piece, piece),
-        in_specs=[SM] + [VM] * 11,
-        out_specs=(VM, VM),
-        scratch_shapes=[pltpu.VMEM((512, PLANE), BF), pltpu.VMEM((288, PLANE), F32)],
-        compiler_params=params,
-    )(zs, *blocks, last_g, low, high, grad_weights)
-
+    last_x = lax.ppermute(a[:, 0], "z", up)
+    last_g = lax.ppermute(b[:, 1], "z", down)
+    core = lax.axis_index("core")
+    info = jnp.stack([z, core]).astype(jnp.int32)
+
+    def call(body, outs, in_specs, scratch=()):
+        return pl.pallas_call(
+            body,
+            out_shape=outs,
+            in_specs=in_specs,
+            out_specs=jax.tree.map(lambda _: VM, outs),
+            scratch_shapes=scratch,
+            compiler_params=pltpu.CompilerParams(vmem_limit_bytes=48 * 1024 * 1024),
+        )
+
+    shape = jax.ShapeDtypeStruct
+    rim = shape((8, 2, 16, PLANE), BF)
+    inner, outer = call(rims_kernel, (rim, rim), [SM] + [VM] * 9)(info, *blocks, last_x, last_g)
+    outer = lax.ppermute(outer, SLAB, [(s, (s + (1 if s % 2 else -1)) % 32) for s in range(32)])
+    inner = lax.ppermute(inner, "core", swap)
+    chunks = call(chunks_kernel, shape((8, 32, 512), BF), [VM, VM, ANY])(pick, flat, inner)
+    turned = lax.all_to_all(chunks, "z", 0, 0, tiled=True)
+
+    piece = shape((16, 2 * PLANE), F32)
+    field = pltpu.VMEM((512, PLANE), BF)
+    prod = pltpu.VMEM((288, PLANE), F32)
+    weights = pltpu.VMEM((288, 384), BF)
+    feat_own, feat_far = call(
+        features_kernel, (piece, piece), [SM] + [VM] * 12, [field, prod, weights]
+    )(info, *blocks, last_x, inner, outer, near, far_filters)
     feat_in = lax.ppermute(feat_far, "yh", swap)
+    filt = call(
+        filter_kernel,
+        shape((2, 16, 8, 432), F32),
+        [SM] + [VM] * 11 + [ANY],
+        [field, pltpu.VMEM((288, 2 * PLANE), BF)],
+    )(info, *blocks, last_x, inner, outer, far, feat_far)
+    got = lax.all_to_all(filt.reshape(32, 8, 432), SLAB, 0, 0, tiled=True)
+    grad_own, grad_far = call(
+        gradient_kernel, (piece, piece), [SM] + [VM] * 11 + [ANY], [field, prod, weights]
+    )(info, *blocks, last_g, inner, outer, turned, filt)
     grad_in = lax.ppermute(grad_far, "yh", swap)
-    got = lax.all_to_all(filt.reshape(32, 8, 432), SLAB, 0, 0, tiled=True)
     factor = 1.0 / math.sqrt(64 * PLANE)
     mine = got.sum(0) * factor
     pairs = []

time: 137 us -> 121 us (0.88)
  the two profiles are of different devices: /device:TPU:19 before, /device:TPU:16 now
where the time goes in v2:
time: 121 us; the launch traced here: 120 us
  starting transfers between devices  80.1 us (66%)
  waiting for transfers between devices  16.4 us (14%)
  Pallas kernels  13 us (11%)
  local copies, waits for them, and re-layouts  6.43 us (5%)
  other arithmetic  3.43 us (3%)
    ppermute x3, starting transfers between devices, local(): b = lax.ppermute(b, 'z', down)  18.9 us
    ppermute x3, starting transfers between devices, local(): a = lax.ppermute(a, 'z', up)  8.23 us
    ppermute x1, starting transfers between devices, local(): feat_in = lax.ppermute(feat_far, 'yh', swap)  6.82 us
    all_to_all x1, starting transfers between devices, local(): got = lax.all_to_all(filt.reshape(32, 8, 432), SLAB, 0, 0, tiled=True)  6.16 us
    ppermute x1, starting transfers between devices, local(): grad_in = lax.ppermute(grad_far, 'yh', swap)  6.11 us
    ppermute x1, starting transfers between devices, local(): far_filters = lax.ppermute(away, 'yh', swap)  5.92 us
    ppermute x1, starting transfers between devices, local(): last_g = lax.ppermute(b[:, 1], 'z', down)  5.61 us
    ppermute x1, starting transfers between devices, local(): lax.ppermute(outer, SLAB, [(s, (s + (1 if s % 2 else -1)) % 32) for s in...  5.55 us
  transfers between devices with their start and end apart: 17, of which 7 were waited for; matrix products, arithmetic and copies ran while one was open for 6% of the time, Pallas kernels for 11%

profile of v2, /device:TPU:16, one launch (start us, length us, event | category | flops | bytes accessed | tf_op | source)
XLA Modules:
  0.0 120.3 jit_solution(4233620376554937300)
XLA Ops:
  0.6 1.0 copy_bitcast_fusion
  1.6 0.0 copy-start
  1.6 0.0 copy-start.3
  1.6 4.4 %collective-permute-start = (bf16[2,2,16,1536]{3,2,0,1:T(8,128)(2,1)S(1)}, bf16[2,2,16,1536]{3,2,0,1:T(8,128)(2,1)S(1)}, u32[]{:S(2)}, u32[]{:S(2)}) collective-permute-start(bf16[2,2,16,1536]{3,2,0,1:T(8,128)(2,1)S(1)} %maximum_bitcast_fusion), channel_id=1, source_target_pairs={{0,1},{1,2},{2,3},{3,4},{4,5},{5,6},{6,7},{7,0},{8,9},{9,10},{10,1... | collective-permute-start | bytes 589832 | tf_op jit(solution)/shard_map/ppermute | solution.py:221
  6.1 8.6 %collective-permute-start.1 = (bf16[2,2,16,1536]{3,2,0,1:T(8,128)(2,1)S(1)}, bf16[2,2,16,1536]{3,2,0,1:T(8,128)(2,1)S(1)}, u32[]{:S(2)}, u32[]{:S(2)}) collective-permute-start(bf16[2,2,16,1536]{3,2,0,1:T(8,128)(2,1)S(1)} %maximum_bitcast_fusion), channel_id=1, source_target_pairs={{0,7},{1,0},{2,1},{3,2},{4,3},{5,4},{6,5},{7,6},{8,15},{9,8},{10,9... | collective-permute-start | bytes 589832 | tf_op jit(solution)/shard_map/ppermute | solution.py:222
  14.7 3.0 %collective-permute-done = bf16[2,2,16,1536]{3,2,0,1:T(8,128)(2,1)S(1)} collective-permute-done((bf16[2,2,16,1536]{3,2,0,1:T(8,128)(2,1)S(1)}, bf16[2,2,16,1536]{3,2,0,1:T(8,128)(2,1)S(1)}, u32[]{:S(2)}, u32[]{:S(2)}) %collective-permute-start) | collective-permute-done | bytes 196640 | tf_op jit(solution)/shard_map/ppermute | solution.py:221
  17.6 1.9 %collective-permute-start.2 = (bf16[2,2,16,1536]{3,2,0,1:T(8,128)(2,1)S(1)}, bf16[2,2,16,1536]{3,2,0,1:T(8,128)(2,1)S(1)}, u32[]{:S(2)}, u32[]{:S(2)}) collective-permute-start(bf16[2,2,16,1536]{3,2,0,1:T(8,128)(2,1)S(1)} %collective-permute-done), channel_id=1, source_target_pairs={{0,1},{1,2},{2,3},{3,4},{4,5},{5,6},{6,7},{7,0},{8,9},{9,10},{10,1... | collective-permute-start | bytes 589832 | tf_op jit(solution)/shard_map/ppermute | solution.py:221
  19.5 0.0 collective-permute-done.1
  19.5 5.1 %collective-permute-start.3 = (bf16[2,2,16,1536]{3,2,0,1:T(8,128)(2,1)S(1)}, bf16[2,2,16,1536]{3,2,0,1:T(8,128)(2,1)S(1)}, u32[]{:S(2)}, u32[]{:S(2)}) collective-permute-start(bf16[2,2,16,1536]{3,2,0,1:T(8,128)(2,1)S(1)} %collective-permute-done.1), channel_id=1, source_target_pairs={{0,7},{1,0},{2,1},{3,2},{4,3},{5,4},{6,5},{7,6},{8,15},{9,8},{10,9... | collective-permute-start | bytes 589832 | tf_op jit(solution)/shard_map/ppermute | solution.py:222
  24.7 2.1 %collective-permute-done.2 = bf16[2,2,16,1536]{3,2,0,1:T(8,128)(2,1)S(1)} collective-permute-done((bf16[2,2,16,1536]{3,2,0,1:T(8,128)(2,1)S(1)}, bf16[2,2,16,1536]{3,2,0,1:T(8,128)(2,1)S(1)}, u32[]{:S(2)}, u32[]{:S(2)}) %collective-permute-start.2) | collective-permute-done | bytes 196640 | tf_op jit(solution)/shard_map/ppermute | solution.py:221
  26.8 1.9 %collective-permute-start.4 = (bf16[2,2,16,1536]{3,2,0,1:T(8,128)(2,1)S(1)}, bf16[2,2,16,1536]{3,2,0,1:T(8,128)(2,1)S(1)}, u32[]{:S(2)}, u32[]{:S(2)}) collective-permute-start(bf16[2,2,16,1536]{3,2,0,1:T(8,128)(2,1)S(1)} %collective-permute-done.2), channel_id=1, source_target_pairs={{0,1},{1,2},{2,3},{3,4},{4,5},{5,6},{6,7},{7,0},{8,9},{9,10},{10,1... | collective-permute-start | bytes 589832 | tf_op jit(solution)/shard_map/ppermute | solution.py:221
  28.7 0.0 copy-done
  28.7 0.7 constant_dynamic-slice_fusion
  29.4 5.9 %collective-permute-start.10 = (bf16[432,128]{1,0:T(8,128)(2,1)}, bf16[432,128]{1,0:T(8,128)(2,1)}, u32[]{:S(2)}, u32[]{:S(2)}) collective-permute-start(bf16[432,128]{1,0:T(8,128)(2,1)} %get-tuple-element.18), channel_id=1, source_target_pairs={{0,8},{8,0},{1,9},{9,1},{2,10},{10,2},{3,11},{11,3},{4,12},{12,4},... | collective-permute-start | bytes 331784 | tf_op jit(solution)/shard_map/ppermute | solution.py:208
  35.3 0.0 collective-permute-done.3
  35.3 5.1 %collective-permute-start.5 = (bf16[2,2,16,1536]{3,2,0,1:T(8,128)(2,1)S(1)}, bf16[2,2,16,1536]{3,2,0,1:T(8,128)(2,1)S(1)}, u32[]{:S(2)}, u32[]{:S(2)}) collective-permute-start(bf16[2,2,16,1536]{3,2,0,1:T(8,128)(2,1)S(1)} %collective-permute-done.3), channel_id=1, source_target_pairs={{0,7},{1,0},{2,1},{3,2},{4,3},{5,4},{6,5},{7,6},{8,15},{9,8},{10,9... | collective-permute-start | bytes 589832 | tf_op jit(solution)/shard_map/ppermute | solution.py:222
  40.5 0.0 collective-permute-done.4
  40.5 1.9 %collective-permute-start.6 = (bf16[2,16,1536]{2,1,0:T(8,128)(2,1)S(1)}, bf16[2,16,1536]{2,1,0:T(8,128)(2,1)S(1)}, u32[]{:S(2)}, u32[]{:S(2)}) collective-permute-start(bf16[2,16,1536]{2,1,0:T(8,128)(2,1)S(1)} %slice_bitcast_fusion.2), channel_id=1, source_target_pairs={{0,1},{1,2},{2,3},{3,4},{4,5},{5,6},{6,7},{7,0},{8,9},{9,10},{10,1... | collective-permute-start | bytes 294920 | tf_op jit(solution)/shard_map/ppermute | solution.py:224
  42.4 1.2 %collective-permute-done.5 = bf16[2,2,16,1536]{3,2,0,1:T(8,128)(2,1)S(1)} collective-permute-done((bf16[2,2,16,1536]{3,2,0,1:T(8,128)(2,1)S(1)}, bf16[2,2,16,1536]{3,2,0,1:T(8,128)(2,1)S(1)}, u32[]{:S(2)}, u32[]{:S(2)}) %collective-permute-start.5) | collective-permute-done | bytes 196640 | tf_op jit(solution)/shard_map/ppermute | solution.py:222
  43.7 0.0 copy-done.3
  43.7 5.6 %collective-permute-start.7 = (bf16[2,16,1536]{2,1,0:T(8,128)(2,1)S(1)}, bf16[2,16,1536]{2,1,0:T(8,128)(2,1)S(1)}, u32[]{:S(2)}, u32[]{:S(2)}) collective-permute-start(bf16[2,16,1536]{2,1,0:T(8,128)(2,1)S(1)} %slice_bitcast_fusion.1), channel_id=1, source_target_pairs={{0,7},{1,0},{2,1},{3,2},{4,3},{5,4},{6,5},{7,6},{8,15},{9,8},{10,9... | collective-permute-start | bytes 294920 | tf_op jit(solution)/shard_map/ppermute | solution.py:225
  49.3 0.1 pad_add_fusion.info
  49.5 0.0 collective-permute-done.6.refs_7_
  49.5 2.0 %collective-permute-done.7.refs_8_.refs_7_ = bf16[2,16,1536]{2,1,0:T(8,128)(2,1)S(1)} collective-permute-done((bf16[2,16,1536]{2,1,0:T(8,128)(2,1)S(1)}, bf16[2,16,1536]{2,1,0:T(8,128)(2,1)S(1)}, u32[]{:S(2)}, u32[]{:S(2)}) %collective-permute-start.7) | collective-permute-done | bytes 98336 | tf_op jit(solution)/shard_map/ppermute | solution.py:225
  51.5 1.5 %shard_map.58 = (bf16[8,2,16,1536]{3,2,1,0:T(8,128)(2,1)S(1)}, bf16[8,2,16,1536]{3,2,1,0:T(8,128)(2,1)}) custom-call(s32[2]{0:T(128)S(1)} %pad_add_fusion.info, bf16[2,2,16,1536]{3,2,1,0:T(8,128)(2,1)S(1)} %copy.45.refs_0_, bf16[2,2,16,1536]{3,2,1,0:T(8,128)(2,1)S(1)} %copy.46.refs_1_, bf16[2,2,16,1536]{3,2,1,0:T(8,128)(2,1)S(1)} %copy.47.refs_2_, ...), custom_call_target="tpu_custom_call" | custom-call | tf_op jit(solution)/shard_map/pallas_call | solution.py:241
  53.0 1.9 %collective-permute-start.8 = (bf16[8,2,16,1536]{3,2,1,0:T(8,128)(2,1)S(1)}, bf16[8,2,16,1536]{3,2,1,0:T(8,128)(2,1)S(1)}, u32[]{:S(2)}, u32[]{:S(2)}) collective-permute-start(bf16[8,2,16,1536]{3,2,1,0:T(8,128)(2,1)S(1)} %get-tuple-element.9), channel_id=1, source_target_pairs={{0,16},{16,0},{1,17},{17,1},{2,18},{18,2},{3,19},{19,3},{4,20},{20... | collective-permute-start | bytes 2359304 | tf_op jit(solution)/shard_map/ppermute | solution.py:243
  55.0 5.6 %collective-permute-start.9 = (bf16[8,2,16,1536]{3,2,1,0:T(8,128)(2,1)}, bf16[8,2,16,1536]{3,2,1,0:T(8,128)(2,1)S(1)}, u32[]{:S(2)}, u32[]{:S(2)}) collective-permute-start(bf16[8,2,16,1536]{3,2,1,0:T(8,128)(2,1)} %get-tuple-element.10), channel_id=1, source_target_pairs={{0,496},{16,32},{32,16},{48,64},{64,48},{80,96},{96,80},{112,128},... | collective-permute-start | bytes 2359304 | tf_op jit(solution)/shard_map/ppermute | solution.py:242
  60.5 0.6 fusion.7.pick
  61.1 0.0 collective-permute-done.8.refs_8_._after
  61.2 1.0 shard_map.60
  62.1 4.9 %all-to-all-start = ((bf16[8,32,512]{2,1,0:T(8,128)(2,1)}), bf16[8,32,512]{2,1,0:T(8,128)(2,1)S(1)}, u32[]{:S(2)}, u32[]{:S(2)}) async-start(bf16[8,32,512]{2,1,0:T(8,128)(2,1)} %shard_map.60), calls=%async_computation | async-start | bytes 524288 | tf_op jit(solution)/shard_map/all_to_all | solution.py:245
  67.0 0.9 slice_bitcast_fusion
  67.9 2.9 %collective-permute-start.12 = (bf16[2,16,1536]{2,1,0:T(8,128)(2,1)S(1)}, bf16[2,16,1536]{2,1,0:T(8,128)(2,1)S(1)}, u32[]{:S(2)}, u32[]{:S(2)}) collective-permute-start(bf16[2,16,1536]{2,1,0:T(8,128)(2,1)S(1)} %slice_bitcast_fusion), channel_id=1, source_target_pairs={{0,8},{8,0},{1,9},{9,1},{2,10},{10,2},{3,11},{11,3},{4,12},{12,4},... | collective-permute-start | bytes 294920 | tf_op jit(solution)/shard_map/ppermute | solution.py:216
  70.8 0.0 collective-permute-done.10.refs_11_
  70.8 0.0 collective-permute-done.9.refs_9_
  70.9 3.1 %shard_map.59 = (f32[16,3072]{1,0:T(8,128)S(1)}, f32[16,3072]{1,0:T(8,128)}) custom-call(s32[2]{0:T(128)S(1)} %pad_add_fusion.info, bf16[2,2,16,1536]{3,2,1,0:T(8,128)(2,1)S(1)} %copy.45.refs_0_, bf16[2,2,16,1536]{3,2,1,0:T(8,128)(2,1)S(1)} %copy.46.refs_1_, bf16[2,2,16,1536]{3,2,1,0:T(8,128)(2,1)S(1)} %copy.47.refs_2_, ...), custom_call_target="tpu_custom_call" | custom-call | tf_op jit(solution)/shard_map/pallas_call | solution.py:251
  74.0 0.0 copy-start.1
  74.0 0.7 copy-done.1
  74.7 6.8 %collective-permute-start.11 = (f32[16,3072]{1,0:T(8,128)}, f32[16,3072]{1,0:T(8,128)}, u32[]{:S(2)}, u32[]{:S(2)}) collective-permute-start(f32[16,3072]{1,0:T(8,128)} %get-tuple-element.12.refs_11_), channel_id=1, source_target_pairs={{0,8},{8,0},{1,9},{9,1},{2,10},{10,2},{3,11},{11,3},{4,12},{12,4},... | collective-permute-start | bytes 589832 | tf_op jit(solution)/shard_map/ppermute | solution.py:254
  81.5 0.0 collective-permute-done.12.refs_10_
  81.5 3.7 %shard_map.61.refs_11_ = f32[2,16,8,432]{3,2,1,0:T(8,128)} custom-call(s32[2]{0:T(128)S(1)} %pad_add_fusion.info, bf16[2,2,16,1536]{3,2,1,0:T(8,128)(2,1)S(1)} %copy.45.refs_0_, bf16[2,2,16,1536]{3,2,1,0:T(8,128)(2,1)S(1)} %copy.46.refs_1_, bf16[2,2,16,1536]{3,2,1,0:T(8,128)(2,1)S(1)} %copy.47.refs_2_, bf16[2,2,16,1536]{3,2,1,0:T(8,128)(2,1)S(1)} %copy.48.refs_3_, ...), custom_call_target="tpu_custom_call" | custom-call | tf_op jit(solution)/shard_map/pallas_call | solution.py:255
  85.3 0.0 all-to-all-done.refs_10_
  85.3 0.0 copy-start.2
  85.3 6.2 %all-to-all-start.1 = ((f32[32,8,432]{2,1,0:T(8,128)}), f32[32,8,432]{2,1,0:T(8,128)}, u32[]{:S(2)}, u32[]{:S(2)}) async-start(f32[32,8,432]{2,1,0:T(8,128)} %bitcast.9), calls=%async_computation.1 | async-start | bytes 1048576 | tf_op jit(solution)/shard_map/all_to_all | solution.py:261
  91.4 0.0 collective-permute-done.11
  91.4 0.0 copy-done.2
  91.5 1.6 %add_convert_fusion.1 = bf16[16,3072]{1,0:T(8,128)(2,1)} fusion(f32[16,3072]{1,0:T(8,128)S(1)} %copy-done.2, f32[16,3072]{1,0:T(8,128)} %collective-permute-done.11), kind=kLoop, calls=%fused_computation.18 | loop fusion | flops 98304 | bytes 491520 | tf_op jit(solution)/shard_map/convert_element_type | solution.py:274
  93.0 1.6 %reshape.22 = bf16[16,2,1536]{2,1,0:T(2,128)(2,1)} reshape(bf16[16,3072]{1,0:T(8,128)(2,1)} %add_convert_fusion.1) | data formatting | bytes 196608 | tf_op jit(solution)/shard_map/reshape | solution.py:274
  94.6 3.6 %shard_map.62 = (f32[16,3072]{1,0:T(8,128)S(1)}, f32[16,3072]{1,0:T(8,128)}) custom-call(s32[2]{0:T(128)S(1)} %pad_add_fusion.info, bf16[2,2,16,1536]{3,2,1,0:T(8,128)(2,1)S(1)} %copy.45.refs_0_, bf16[2,2,16,1536]{3,2,1,0:T(8,128)(2,1)S(1)} %copy.46.refs_1_, bf16[2,2,16,1536]{3,2,1,0:T(8,128)(2,1)S(1)} %copy.47.refs_2_, ...), custom_call_target="tpu_custom_call" | custom-call | tf_op jit(solution)/shard_map/pallas_call | solution.py:262
  98.2 6.1 %collective-permute-start.13 = (f32[16,3072]{1,0:T(8,128)}, f32[16,3072]{1,0:T(8,128)S(1)}, u32[]{:S(2)}, u32[]{:S(2)}) collective-permute-start(f32[16,3072]{1,0:T(8,128)} %get-tuple-element.14), channel_id=1, source_target_pairs={{0,8},{8,0},{1,9},{9,1},{2,10},{10,2},{3,11},{11,3},{4,12},{12,4},... | collective-permute-start | bytes 589832 | tf_op jit(solution)/shard_map/ppermute | solution.py:265
  104.3 1.9 %all-to-all-done.1 = f32[32,8,432]{2,1,0:T(8,128)} async-done(((f32[32,8,432]{2,1,0:T(8,128)}), f32[32,8,432]{2,1,0:T(8,128)}, u32[]{:S(2)}, u32[]{:S(2)}) %all-to-all-start.1) | async-done | bytes 442400 | tf_op jit(solution)/shard_map/all_to_all | solution.py:261
  106.2 1.1 reduce_sum.9
  107.3 5.2 %collective-permute-start.14 = (f32[8,432]{1,0:T(8,128)S(1)}, f32[8,432]{1,0:T(8,128)S(1)}, u32[]{:S(2)}, u32[]{:S(2)}) collective-permute-start(f32[8,432]{1,0:T(8,128)S(1)} %broadcast_multiply_fusion), channel_id=1, source_target_pairs={{0,0},{8,264},{256,8},{264,256},{1,1},{9,265},{257,9},{265,257},{2... | collective-permute-start | bytes 41480 | tf_op jit(solution)/shard_map/ppermute | solution.py:272
  112.5 3.4 %collective-permute-done.13 = f32[16,3072]{1,0:T(8,128)S(1)} collective-permute-done((f32[16,3072]{1,0:T(8,128)}, f32[16,3072]{1,0:T(8,128)S(1)}, u32[]{:S(2)}, u32[]{:S(2)}) %collective-permute-start.13) | collective-permute-done | bytes 196640 | tf_op jit(solution)/shard_map/ppermute | solution.py:265
  115.9 0.7 reshape.23
  116.6 2.8 %collective-permute-done.14 = f32[8,432]{1,0:T(8,128)S(1)} collective-permute-done((f32[8,432]{1,0:T(8,128)S(1)}, f32[8,432]{1,0:T(8,128)S(1)}, u32[]{:S(2)}, u32[]{:S(2)}) %collective-permute-start.14) | collective-permute-done | bytes 13856 | tf_op jit(solution)/shard_map/ppermute | solution.py:272
  119.4 0.1 reshape.25
  119.5 0.7 copy.66
  (17 shorter events, 0.2 us)
Async XLA Ops:
  1.6 27.1 %copy-start = (bf16[27,16,256]{2,1,0:T(8,128)(2,1)S(1)}, bf16[27,16,256]{2,1,0:T(8,128)(2,1)}, u32[]{:S(2)}) copy-start(bf16[27,16,256]{2,1,0:T(8,128)(2,1)} %param.4) | copy-start | bytes 663556
  1.6 42.0 %copy-start.3 = (bf16[2,2,16,1536]{3,2,0,1:T(8,128)(2,1)}, bf16[2,2,16,1536]{3,2,0,1:T(8,128)(2,1)S(1)}, u32[]{:S(2)}) copy-start(bf16[2,2,16,1536]{3,2,0,1:T(8,128)(2,1)S(1)} %maximum_bitcast_fusion) | copy-start | bytes 589828
  1.6 16.0 %collective-permute-start = (bf16[2,2,16,1536]{3,2,0,1:T(8,128)(2,1)S(1)}, bf16[2,2,16,1536]{3,2,0,1:T(8,128)(2,1)S(1)}, u32[]{:S(2)}, u32[]{:S(2)}) collective-permute-start(bf16[2,2,16,1536]{3,2,0,1:T(8,128)(2,1)S(1)} %maximum_bitcast_fusion), channel_id=1, source_target_pairs={{0,1},{1,2},{2,3},{3,4},{4,5},{5,6},{6,7},{7,0},{8,9},{9,10},{10,1... | collective-permute-start | bytes 589832 | tf_op jit(solution)/shard_map/ppermute | solution.py:221
  6.1 13.5 %collective-permute-start.1 = (bf16[2,2,16,1536]{3,2,0,1:T(8,128)(2,1)S(1)}, bf16[2,2,16,1536]{3,2,0,1:T(8,128)(2,1)S(1)}, u32[]{:S(2)}, u32[]{:S(2)}) collective-permute-start(bf16[2,2,16,1536]{3,2,0,1:T(8,128)(2,1)S(1)} %maximum_bitcast_fusion), channel_id=1, source_target_pairs={{0,7},{1,0},{2,1},{3,2},{4,3},{5,4},{6,5},{7,6},{8,15},{9,8},{10,9... | collective-permute-start | bytes 589832 | tf_op jit(solution)/shard_map/ppermute | solution.py:222
  17.6 9.2 %collective-permute-start.2 = (bf16[2,2,16,1536]{3,2,0,1:T(8,128)(2,1)S(1)}, bf16[2,2,16,1536]{3,2,0,1:T(8,128)(2,1)S(1)}, u32[]{:S(2)}, u32[]{:S(2)}) collective-permute-start(bf16[2,2,16,1536]{3,2,0,1:T(8,128)(2,1)S(1)} %collective-permute-done), channel_id=1, source_target_pairs={{0,1},{1,2},{2,3},{3,4},{4,5},{5,6},{6,7},{7,0},{8,9},{9,10},{10,1... | collective-permute-start | bytes 589832 | tf_op jit(solution)/shard_map/ppermute | solution.py:221
  19.5 15.8 %collective-permute-start.3 = (bf16[2,2,16,1536]{3,2,0,1:T(8,128)(2,1)S(1)}, bf16[2,2,16,1536]{3,2,0,1:T(8,128)(2,1)S(1)}, u32[]{:S(2)}, u32[]{:S(2)}) collective-permute-start(bf16[2,2,16,1536]{3,2,0,1:T(8,128)(2,1)S(1)} %collective-permute-done.1), channel_id=1, source_target_pairs={{0,7},{1,0},{2,1},{3,2},{4,3},{5,4},{6,5},{7,6},{8,15},{9,8},{10,9... | collective-permute-start | bytes 589832 | tf_op jit(solution)/shard_map/ppermute | solution.py:222
  26.8 13.7 %collective-permute-start.4 = (bf16[2,2,16,1536]{3,2,0,1:T(8,128)(2,1)S(1)}, bf16[2,2,16,1536]{3,2,0,1:T(8,128)(2,1)S(1)}, u32[]{:S(2)}, u32[]{:S(2)}) collective-permute-start(bf16[2,2,16,1536]{3,2,0,1:T(8,128)(2,1)S(1)} %collective-permute-done.2), channel_id=1, source_target_pairs={{0,1},{1,2},{2,3},{3,4},{4,5},{5,6},{6,7},{7,0},{8,9},{9,10},{10,1... | collective-permute-start | bytes 589832 | tf_op jit(solution)/shard_map/ppermute | solution.py:221
  29.4 41.5 %collective-permute-start.10 = (bf16[432,128]{1,0:T(8,128)(2,1)}, bf16[432,128]{1,0:T(8,128)(2,1)}, u32[]{:S(2)}, u32[]{:S(2)}) collective-permute-start(bf16[432,128]{1,0:T(8,128)(2,1)} %get-tuple-element.18), channel_id=1, source_target_pairs={{0,8},{8,0},{1,9},{9,1},{2,10},{10,2},{3,11},{11,3},{4,12},{12,4},... | collective-permute-start | bytes 331784 | tf_op jit(solution)/shard_map/ppermute | solution.py:208
  35.3 8.3 %collective-permute-start.5 = (bf16[2,2,16,1536]{3,2,0,1:T(8,128)(2,1)S(1)}, bf16[2,2,16,1536]{3,2,0,1:T(8,128)(2,1)S(1)}, u32[]{:S(2)}, u32[]{:S(2)}) collective-permute-start(bf16[2,2,16,1536]{3,2,0,1:T(8,128)(2,1)S(1)} %collective-permute-done.3), channel_id=1, source_target_pairs={{0,7},{1,0},{2,1},{3,2},{4,3},{5,4},{6,5},{7,6},{8,15},{9,8},{10,9... | collective-permute-start | bytes 589832 | tf_op jit(solution)/shard_map/ppermute | solution.py:222
  40.5 9.0 %collective-permute-start.6 = (bf16[2,16,1536]{2,1,0:T(8,128)(2,1)S(1)}, bf16[2,16,1536]{2,1,0:T(8,128)(2,1)S(1)}, u32[]{:S(2)}, u32[]{:S(2)}) collective-permute-start(bf16[2,16,1536]{2,1,0:T(8,128)(2,1)S(1)} %slice_bitcast_fusion.2), channel_id=1, source_target_pairs={{0,1},{1,2},{2,3},{3,4},{4,5},{5,6},{6,7},{7,0},{8,9},{9,10},{10,1... | collective-permute-start | bytes 294920 | tf_op jit(solution)/shard_map/ppermute | solution.py:224
  43.7 7.8 %collective-permute-start.7 = (bf16[2,16,1536]{2,1,0:T(8,128)(2,1)S(1)}, bf16[2,16,1536]{2,1,0:T(8,128)(2,1)S(1)}, u32[]{:S(2)}, u32[]{:S(2)}) collective-permute-start(bf16[2,16,1536]{2,1,0:T(8,128)(2,1)S(1)} %slice_bitcast_fusion.1), channel_id=1, source_target_pairs={{0,7},{1,0},{2,1},{3,2},{4,3},{5,4},{6,5},{7,6},{8,15},{9,8},{10,9... | collective-permute-start | bytes 294920 | tf_op jit(solution)/shard_map/ppermute | solution.py:225
  53.0 8.1 %collective-permute-start.8 = (bf16[8,2,16,1536]{3,2,1,0:T(8,128)(2,1)S(1)}, bf16[8,2,16,1536]{3,2,1,0:T(8,128)(2,1)S(1)}, u32[]{:S(2)}, u32[]{:S(2)}) collective-permute-start(bf16[8,2,16,1536]{3,2,1,0:T(8,128)(2,1)S(1)} %get-tuple-element.9), channel_id=1, source_target_pairs={{0,16},{16,0},{1,17},{17,1},{2,18},{18,2},{3,19},{19,3},{4,20},{20... | collective-permute-start | bytes 2359304 | tf_op jit(solution)/shard_map/ppermute | solution.py:243
  55.0 15.9 %collective-permute-start.9 = (bf16[8,2,16,1536]{3,2,1,0:T(8,128)(2,1)}, bf16[8,2,16,1536]{3,2,1,0:T(8,128)(2,1)S(1)}, u32[]{:S(2)}, u32[]{:S(2)}) collective-permute-start(bf16[8,2,16,1536]{3,2,1,0:T(8,128)(2,1)} %get-tuple-element.10), channel_id=1, source_target_pairs={{0,496},{16,32},{32,16},{48,64},{64,48},{80,96},{96,80},{112,128},... | collective-permute-start | bytes 2359304 | tf_op jit(solution)/shard_map/ppermute | solution.py:242
  62.1 23.1 %all-to-all-start = ((bf16[8,32,512]{2,1,0:T(8,128)(2,1)}), bf16[8,32,512]{2,1,0:T(8,128)(2,1)S(1)}, u32[]{:S(2)}, u32[]{:S(2)}) async-start(bf16[8,32,512]{2,1,0:T(8,128)(2,1)} %shard_map.60), calls=%async_computation | async-start | bytes 524288 | tf_op jit(solution)/shard_map/all_to_all | solution.py:245
  67.9 13.6 %collective-permute-start.12 = (bf16[2,16,1536]{2,1,0:T(8,128)(2,1)S(1)}, bf16[2,16,1536]{2,1,0:T(8,128)(2,1)S(1)}, u32[]{:S(2)}, u32[]{:S(2)}) collective-permute-start(bf16[2,16,1536]{2,1,0:T(8,128)(2,1)S(1)} %slice_bitcast_fusion), channel_id=1, source_target_pairs={{0,8},{8,0},{1,9},{9,1},{2,10},{10,2},{3,11},{11,3},{4,12},{12,4},... | collective-permute-start | bytes 294920 | tf_op jit(solution)/shard_map/ppermute | solution.py:216
  74.0 0.7 copy-start.1
  74.7 16.8 %collective-permute-start.11 = (f32[16,3072]{1,0:T(8,128)}, f32[16,3072]{1,0:T(8,128)}, u32[]{:S(2)}, u32[]{:S(2)}) collective-permute-start(f32[16,3072]{1,0:T(8,128)} %get-tuple-element.12.refs_11_), channel_id=1, source_target_pairs={{0,8},{8,0},{1,9},{9,1},{2,10},{10,2},{3,11},{11,3},{4,12},{12,4},... | collective-permute-start | bytes 589832 | tf_op jit(solution)/shard_map/ppermute | solution.py:254
  85.3 6.2 %copy-start.2 = (f32[16,3072]{1,0:T(8,128)S(1)}, f32[16,3072]{1,0:T(8,128)}, u32[]{:S(2)}) copy-start(f32[16,3072]{1,0:T(8,128)} %copy-done.1) | copy-start | bytes 589828
  85.3 20.9 %all-to-all-start.1 = ((f32[32,8,432]{2,1,0:T(8,128)}), f32[32,8,432]{2,1,0:T(8,128)}, u32[]{:S(2)}, u32[]{:S(2)}) async-start(f32[32,8,432]{2,1,0:T(8,128)} %bitcast.9), calls=%async_computation.1 | async-start | bytes 1048576 | tf_op jit(solution)/shard_map/all_to_all | solution.py:261
  98.2 17.7 %collective-permute-start.13 = (f32[16,3072]{1,0:T(8,128)}, f32[16,3072]{1,0:T(8,128)S(1)}, u32[]{:S(2)}, u32[]{:S(2)}) collective-permute-start(f32[16,3072]{1,0:T(8,128)} %get-tuple-element.14), channel_id=1, source_target_pairs={{0,8},{8,0},{1,9},{9,1},{2,10},{10,2},{3,11},{11,3},{4,12},{12,4},... | collective-permute-start | bytes 589832 | tf_op jit(solution)/shard_map/ppermute | solution.py:265
  107.3 12.1 %collective-permute-start.14 = (f32[8,432]{1,0:T(8,128)S(1)}, f32[8,432]{1,0:T(8,128)S(1)}, u32[]{:S(2)}, u32[]{:S(2)}) collective-permute-start(f32[8,432]{1,0:T(8,128)S(1)} %broadcast_multiply_fusion), channel_id=1, source_target_pairs={{0,0},{8,264},{256,8},{264,256},{1,1},{9,265},{257,9},{265,257},{2... | collective-permute-start | bytes 41480 | tf_op jit(solution)/shard_map/ppermute | solution.py:272

commit v3 on v2

v3 whole, which is shorter than its diff:
```python
import math

import jax
import jax.numpy as jnp
from jax import lax
from jax.experimental import pallas as pl
from jax.experimental.pallas import tpu as pltpu
from jax.sharding import Mesh, PartitionSpec as P


AXES = ("yl1", "yl0", "x", "core", "yh", "z")
SIZES = (2, 2, 4, 2, 2, 8)
PLANE = 1536
BF = jnp.bfloat16
F32 = jnp.float32
SLAB = ("yl1", "yl0", "x", "core")
RING = (0, -1, 1, -2, 2, -3, 3, 4)


def shift_pairs(size, step):
    return [(i, (i + step) % size) for i in range(size)]


def shift_add(rows, sign):
    lane = lax.broadcasted_iota(jnp.int32, (16, 128), 1)
    low = lane < 64
    edge_up = (lane % 64) == 63
    edge_down = (lane % 64) == 0
    count = PLANE // 128
    out = [None] * count
    for r in (-1, 0, 1):
        step = sign * r
        total = []
        taps = []
        for q in (-1, 0, 1):
            v = rows(3 * (q + 1) + r + 1)
            taps.append([v[:, 128 * i : 128 * i + 128] for i in range(count)])
        by_step = {sign * q: taps[q + 1] for q in (-1, 0, 1)}
        up = [pltpu.roll(v, 64, 1) for v in by_step[1]]
        down = [pltpu.roll(v, 64, 1) for v in by_step[-1]]
        for i in range(count):
            a = jnp.where(low, up[i], up[(i + 1) % count])
            b = jnp.where(low, down[(i - 1) % count], down[i])
            total.append(by_step[0][i] + a + b)
        for i in range(count):
            v = total[i]
            if step == 1:
                v = jnp.where(edge_up, pltpu.roll(v, 63, 1), pltpu.roll(v, 127, 1))
            elif step == -1:
                v = jnp.where(edge_down, pltpu.roll(v, 65, 1), pltpu.roll(v, 1, 1))
            out[i] = v if out[i] is None else out[i] + v
    return out


def gather_blocks(info, part, blocks, inner, outer, field):
    z, core = info[0], info[1]
    inner_at, outer_at = (1 - core) * 384, core * 384
    for j, off in enumerate(RING):
        row = pl.multiple_of(lax.rem(z + off + 8, 8) * 16, 16)
        for d in range(2):
            field[pl.ds((d + 1) * 128 + row, 16), :] = blocks[j][d, part]
        field[pl.ds(pl.multiple_of(inner_at + row, 16), 16), :] = inner[j, part]
        field[pl.ds(pl.multiple_of(outer_at + row, 16), 16), :] = outer[j]


def conv(field, weights, prod, out_own, out_far, sign):
    for d in range(2):
        prod[...] = jnp.dot(
            weights[...], field[pl.ds(d * 128, 384), :], preferred_element_type=F32
        )
        for m, out in enumerate((out_own, out_far)):
            cols = shift_add(lambda k: prod[pl.ds(m * 144 + k * 16, 16), :], sign)
            for i, v in enumerate(cols):
                out[:, pl.ds(d * PLANE + i * 128, 128)] = v


def grad_weights(turned, weights):
    lane = lax.broadcasted_iota(jnp.int32, (32, 128), 1) // 16
    got = [turned[k].astype(F32) for k in range(8)]
    for t in range(27):
        p, qr = t // 9, t % 9
        lo = t * 16 // 128 * 128
        total = None
        for k in range(8):
            v = got[k][:, lo : lo + 128]
            v = pltpu.roll(v, (16 * k - (t * 16 - lo)) % 128, 1)
            total = v if total is None else jnp.where(lane == k, v, total)
        total = total.astype(BF)
        for m in range(2):
            weights[pl.ds(m * 144 + qr * 16, 16), pl.ds((2 - p) * 128, 128)] = total[
                16 * m : 16 * m + 16
            ]


def rims_kernel(info, *refs):
    ring, (inner, outer_x, outer_g) = refs[:8], refs[8:]
    core = info[1]
    for j in range(8):
        inner[j] = ring[j][1 - core]
        outer_x[j] = ring[j][core, 0]
        outer_g[j] = ring[j][core, 1]


def fold_kernel(info, got, out):
    yh = info[2]
    sums = []
    for k in range(4):
        v = got[0, k]
        for i in range(1, 8):
            v = v + got[i, k]
        sums.append(v)
    for a in range(2):
        for b in range(2):
            for h in range(2):
                v = jnp.where(yh == 0, sums[h * 2 + b], sums[(1 - h) * 2 + b])
                out[(a * 2 + b) * 2 + h] = jnp.where(yh == a, v, jnp.zeros_like(v))


def pack_kernel(info, own, flat, *refs):
    out = refs[-1]
    out[pl.ds(0, 432), :] = flat[:, pl.ds(pl.multiple_of((1 - info[2]) * 128, 128), 128)]
    for d in range(2):
        for i in range(PLANE // 128):
            out[pl.ds(432 + (d * 12 + i) * 16, 16), :] = own[d, 1, :, pl.ds(i * 128, 128)]


def features_kernel(info, *refs):
    ring, (inner, outer, flat, packed) = refs[:8], refs[8:12]
    out_own, out_far, field, prod, weights = refs[12:]
    gather_blocks(info, 0, ring, inner, outer, field)
    half = pl.ds(pl.multiple_of(info[2] * 128, 128), 128)
    for p in range(3):
        rows, cols = pl.ds(p * 144, 144), pl.ds(p * 128, 128)
        weights[pl.ds(0, 144), cols] = flat[rows, half]
        weights[pl.ds(144, 144), cols] = packed[rows, :]
    conv(field, weights, prod, out_own, out_far, 1)


def filter_kernel(info, *refs):
    ring, (inner, outer, packed) = refs[:8], refs[8:11]
    out_filter, field, shifted = refs[11:]
    gather_blocks(info, 0, ring, inner, outer, field)
    filter_part(ring[0], packed, field, shifted, out_filter)


def gradient_kernel(info, *refs):
    ring, (inner, outer, turned) = refs[:8], refs[8:11]
    out_own, out_far, field, prod, weights = refs[11:]
    gather_blocks(info, 1, ring, inner, outer, field)
    grad_weights(turned, weights)
    conv(field, weights, prod, out_own, out_far, -1)


def chunks_kernel(pick, flat, out):
    v = lax.dot_general(
        pick[...], flat[...], (((1,), (1,)), ((), ())), preferred_element_type=F32
    ).astype(BF)
    for k in range(8):
        out[k, :, pl.ds(0, 432)] = v[32 * k : 32 * k + 32]
        out[k, :, pl.ds(432, 80)] = jnp.zeros((32, 80), BF)


def filter_part(own, packed, x_field, shifted, out_filter):
    lane = lax.broadcasted_iota(jnp.int32, (16, 128), 1)
    left = lane < 64
    edge_up = (lane % 64) == 63
    edge_down = (lane % 64) == 0
    count = PLANE // 128
    for m in range(2):
        for d in range(2):
            if m == 0:
                base = [own[d, 1, :, pl.ds(128 * i, 128)] for i in range(count)]
            else:
                base = [packed[pl.ds(432 + (d * 12 + i) * 16, 16), :] for i in range(count)]
            base = [v.astype(F32) for v in base]
            for r in (-1, 0, 1):
                if r == 0:
                    col = base
                elif r == 1:
                    col = [jnp.where(edge_down, pltpu.roll(a, 65, 1), pltpu.roll(a, 1, 1)) for a in base]
                else:
                    col = [jnp.where(edge_up, pltpu.roll(a, 63, 1), pltpu.roll(a, 127, 1)) for a in base]
                half = [pltpu.roll(a, 64, 1) for a in col]
                for q in (-1, 0, 1):
                    row = m * 144 + (3 * (q + 1) + r + 1) * 16
                    for i in range(count):
                        if q == 0:
                            a = col[i]
                        elif q == 1:
                            a = jnp.where(left, half[(i - 1) % count], half[i])
                        else:
                            a = jnp.where(left, half[i], half[(i + 1) % count])
                        shifted[pl.ds(row, 16), pl.ds(d * PLANE + i * 128, 128)] = a.astype(BF)
    total = None
    for d in range(2):
        part = lax.dot_general(
            x_field[pl.ds(d * 128, 384), :],
            shifted[:, pl.ds(d * PLANE, PLANE)],
            (((1,), (1,)), ((), ())),
            preferred_element_type=F32,
        )
        total = part if total is None else total + part
    for m in range(2):
        for yl0 in range(2):
            for p in range(3):
                row = p * 128 + yl0 * 64
                out_filter[:, m * 2 + yl0, :, pl.ds(p * 144, 144)] = total[
                    row : row + 64, m * 144 : m * 144 + 144
                ].reshape(8, 8, 144)


VM = pl.BlockSpec(memory_space=pltpu.VMEM)
SM = pl.BlockSpec(memory_space=pltpu.SMEM)


def call(body, outs, in_specs, scratch=()):
    return pl.pallas_call(
        body,
        out_shape=outs,
        in_specs=in_specs,
        out_specs=jax.tree.map(lambda _: VM, outs),
        scratch_shapes=scratch,
        compiler_params=pltpu.CompilerParams(vmem_limit_bytes=48 * 1024 * 1024),
    )


def run(inputs, filters, cotangent):
    z, yh, core = lax.axis_index("z"), lax.axis_index("yh"), lax.axis_index("core")
    info = jnp.stack([z, core, yh]).astype(jnp.int32)
    shape = jax.ShapeDtypeStruct
    swap = [(0, 1), (1, 0)]
    flat = filters.reshape(432, 256)

    own = jnp.stack([inputs, cotangent]).transpose(2, 0, 1, 3)
    up, down = shift_pairs(8, 1), shift_pairs(8, -1)
    blocks = [own]
    a = b = own
    for _ in range(3):
        a = lax.ppermute(a, "z", up)
        b = lax.ppermute(b, "z", down)
        blocks += [a, b]
    blocks.append(lax.ppermute(own, "z", shift_pairs(8, 4)))

    packed = call(pack_kernel, shape((816, 128), BF), [SM, VM, VM])(info, own, flat)
    packed = lax.ppermute(packed, "yh", swap)

    rim = shape((8, 2, 16, PLANE), BF)
    half = shape((8, 16, PLANE), BF)
    inner, outer_x, outer_g = call(rims_kernel, (rim, half, half), [SM] + [VM] * 8)(info, *blocks)
    outer_pairs = [(s, (s + (1 if s % 2 else -1)) % 32) for s in range(32)]
    outer_x = lax.ppermute(outer_x, SLAB, outer_pairs)
    outer_g = lax.ppermute(outer_g, SLAB, outer_pairs)
    inner = lax.ppermute(inner, "core", swap)

    row = lax.broadcasted_iota(jnp.int32, (256, 256), 0)
    col = lax.broadcasted_iota(jnp.int32, (256, 256), 1)
    zz, m, i = row // 32, (row // 16) % 2, row % 16
    wanted = ((yh + m) % 2) * 128 + zz * 16 + i
    pick = (col == wanted).astype(BF)
    chunks = call(chunks_kernel, shape((8, 32, 512), BF), [VM, VM])(pick, flat)
    turned = lax.all_to_all(chunks, "z", 0, 0, tiled=True)

    piece = shape((16, 2 * PLANE), F32)
    field = pltpu.VMEM((512, PLANE), BF)
    prod = pltpu.VMEM((288, PLANE), F32)
    weights = pltpu.VMEM((288, 384), BF)
    filt = call(
        filter_kernel,
        shape((8, 4, 8, 432), F32),
        [SM] + [VM] * 11,
        [field, pltpu.VMEM((288, 2 * PLANE), BF)],
    )(info, *blocks, inner, outer_x, packed)
    got = lax.all_to_all(filt, ("x", "core"), 0, 0, tiled=True)
    feat_own, feat_far = call(
        features_kernel, (piece, piece), [SM] + [VM] * 12, [field, prod, weights]
    )(info, *blocks, inner, outer_x, flat, packed)
    feat_in = lax.ppermute(feat_far, "yh", swap)
    grad_own, grad_far = call(
        gradient_kernel, (piece, piece), [SM] + [VM] * 11, [field, prod, weights]
    )(info, *blocks, inner, outer_g, turned)
    grad_in = lax.ppermute(grad_far, "yh", swap)

    got = call(fold_kernel, shape((8, 8, 432), F32), [SM, VM])(info, got)
    got = lax.all_to_all(got, ("yl1", "yl0", "yh"), 0, 0, tiled=True)
    mine = got.sum(0) * (1.0 / math.sqrt(64 * PLANE))
    filter_grad = mine.reshape(8, 27, 16).transpose(1, 2, 0)
    features = (feat_own + feat_in).astype(BF).reshape(16, 2, PLANE)
    input_grad = (grad_own + grad_in).astype(BF).reshape(16, 2, PLANE)
    return features, input_grad, filter_grad


def solution(mesh):
    fine = Mesh(mesh.devices.reshape(SIZES), AXES)
    chan = ("yh", "z")
    field = P(chan, SLAB, None)
    return jax.shard_map(
        run,
        mesh=fine,
        in_specs=(field, P(None, chan, None), field),
        out_specs=(field, field, P(None, chan, SLAB)),
        check_vma=False,
    )
```

time: 121 us -> 129 us (1.066)
  the two profiles are of different devices: /device:TPU:16 before, /device:TPU:8 now
where the time goes in v3:
time: 129 us; the launch traced here: 128 us
  starting transfers between devices  76.7 us (59%)
  waiting for transfers between devices  30 us (23%)
  Pallas kernels  15.1 us (12%)
  local copies, waits for them, and re-layouts  3.86 us (3%)
  other arithmetic  1.72 us (1%)
    ppermute x3, starting transfers between devices, run(): b = lax.ppermute(b, 'z', down)  19.5 us
    all_to_all x1, waiting for transfers between devices, run(): got = lax.all_to_all(filt, ('x', 'core'), 0, 0, tiled=True)  9.35 us
    ppermute x3, starting transfers between devices, run(): a = lax.ppermute(a, 'z', up)  8.11 us
    ppermute x1, starting transfers between devices, run(): packed = lax.ppermute(packed, 'yh', swap)  7.73 us
    all_to_all x1, starting transfers between devices, run(): got = lax.all_to_all(got, ('yl1', 'yl0', 'yh'), 0, 0, tiled=True)  7.32 us
    ppermute x1, starting transfers between devices, run(): feat_in = lax.ppermute(feat_far, 'yh', swap)  7.04 us
    ppermute x3, waiting for transfers between devices, run(): b = lax.ppermute(b, 'z', down)  6.86 us
    all_to_all x1, starting transfers between devices, run(): got = lax.all_to_all(filt, ('x', 'core'), 0, 0, tiled=True)  6.1 us
  transfers between devices with their start and end apart: 16, of which 7 were waited for; matrix products, arithmetic and copies ran while one was open for 2% of the time, Pallas kernels for 10%

profile of v3, /device:TPU:8, one launch (start us, length us, event | category | flops | bytes accessed | tf_op | source)
XLA Modules:
  0.0 128.4 jit_solution(18217980322595782235)
XLA Ops:
  0.6 1.0 copy_bitcast_fusion
  1.6 4.3 %collective-permute-start = (bf16[2,2,16,1536]{3,2,1,0:T(8,128)(2,1)S(1)}, bf16[2,2,16,1536]{3,2,1,0:T(8,128)(2,1)S(1)}, u32[]{:S(2)}, u32[]{:S(2)}) collective-permute-start(bf16[2,2,16,1536]{3,2,1,0:T(8,128)(2,1)S(1)} %maximum_bitcast_fusion.refs_0_.own), channel_id=1, source_target_pairs={{0,1},{1,2},{2,3},{3,4},{4,5},{5,6},{6,7},{7,0},{8,9},{9,10},{10,1... | collective-permute-start | bytes 589832 | tf_op jit(solution)/shard_map/ppermute | solution.py:239
  5.9 8.6 %collective-permute-start.1 = (bf16[2,2,16,1536]{3,2,1,0:T(8,128)(2,1)S(1)}, bf16[2,2,16,1536]{3,2,1,0:T(8,128)(2,1)S(1)}, u32[]{:S(2)}, u32[]{:S(2)}) collective-permute-start(bf16[2,2,16,1536]{3,2,1,0:T(8,128)(2,1)S(1)} %maximum_bitcast_fusion.refs_0_.own), channel_id=1, source_target_pairs={{0,7},{1,0},{2,1},{3,2},{4,3},{5,4},{6,5},{7,6},{8,15},{9,8},{10,9... | collective-permute-start | bytes 589832 | tf_op jit(solution)/shard_map/ppermute | solution.py:240
  14.5 3.0 %collective-permute-done.refs_1_ = bf16[2,2,16,1536]{3,2,1,0:T(8,128)(2,1)S(1)} collective-permute-done((bf16[2,2,16,1536]{3,2,1,0:T(8,128)(2,1)S(1)}, bf16[2,2,16,1536]{3,2,1,0:T(8,128)(2,1)S(1)}, u32[]{:S(2)}, u32[]{:S(2)}) %collective-permute-start) | collective-permute-done | bytes 196640 | tf_op jit(solution)/shard_map/ppermute | solution.py:239
  17.5 1.9 %collective-permute-start.2 = (bf16[2,2,16,1536]{3,2,1,0:T(8,128)(2,1)S(1)}, bf16[2,2,16,1536]{3,2,1,0:T(8,128)(2,1)S(1)}, u32[]{:S(2)}, u32[]{:S(2)}) collective-permute-start(bf16[2,2,16,1536]{3,2,1,0:T(8,128)(2,1)S(1)} %collective-permute-done.refs_1_), channel_id=1, source_target_pairs={{0,1},{1,2},{2,3},{3,4},{4,5},{5,6},{6,7},{7,0},{8,9},{9,10},{10,1... | collective-permute-start | bytes 589832 | tf_op jit(solution)/shard_map/ppermute | solution.py:239
  19.4 0.0 collective-permute-done.1.refs_2_
  19.4 5.1 %collective-permute-start.3 = (bf16[2,2,16,1536]{3,2,1,0:T(8,128)(2,1)S(1)}, bf16[2,2,16,1536]{3,2,1,0:T(8,128)(2,1)S(1)}, u32[]{:S(2)}, u32[]{:S(2)}) collective-permute-start(bf16[2,2,16,1536]{3,2,1,0:T(8,128)(2,1)S(1)} %collective-permute-done.1.refs_2_), channel_id=1, source_target_pairs={{0,7},{1,0},{2,1},{3,2},{4,3},{5,4},{6,5},{7,6},{8,15},{9,8},{10,9... | collective-permute-start | bytes 589832 | tf_op jit(solution)/shard_map/ppermute | solution.py:240
  24.5 4.8 %collective-permute-start.6 = (bf16[2,2,16,1536]{3,2,1,0:T(8,128)(2,1)S(1)}, bf16[2,2,16,1536]{3,2,1,0:T(8,128)(2,1)S(1)}, u32[]{:S(2)}, u32[]{:S(2)}) collective-permute-start(bf16[2,2,16,1536]{3,2,1,0:T(8,128)(2,1)S(1)} %maximum_bitcast_fusion.refs_0_.own), channel_id=1, source_target_pairs={{0,4},{1,5},{2,6},{3,7},{4,0},{5,1},{6,2},{7,3},{8,12},{9,13},{10,... | collective-permute-start | bytes 589832 | tf_op jit(solution)/shard_map/ppermute | solution.py:242
  29.4 0.0 collective-permute-done.2.refs_3_
  29.4 1.9 %collective-permute-start.4 = (bf16[2,2,16,1536]{3,2,1,0:T(8,128)(2,1)S(1)}, bf16[2,2,16,1536]{3,2,1,0:T(8,128)(2,1)S(1)}, u32[]{:S(2)}, u32[]{:S(2)}) collective-permute-start(bf16[2,2,16,1536]{3,2,1,0:T(8,128)(2,1)S(1)} %collective-permute-done.2.refs_3_), channel_id=1, source_target_pairs={{0,1},{1,2},{2,3},{3,4},{4,5},{5,6},{6,7},{7,0},{8,9},{9,10},{10,1... | collective-permute-start | bytes 589832 | tf_op jit(solution)/shard_map/ppermute | solution.py:239
  31.3 4.1 %collective-permute-done.3.refs_4_ = bf16[2,2,16,1536]{3,2,1,0:T(8,128)(2,1)S(1)} collective-permute-done((bf16[2,2,16,1536]{3,2,1,0:T(8,128)(2,1)S(1)}, bf16[2,2,16,1536]{3,2,1,0:T(8,128)(2,1)S(1)}, u32[]{:S(2)}, u32[]{:S(2)}) %collective-permute-start.3) | collective-permute-done | bytes 196640 | tf_op jit(solution)/shard_map/ppermute | solution.py:240
  35.4 5.7 %collective-permute-start.5 = (bf16[2,2,16,1536]{3,2,1,0:T(8,128)(2,1)S(1)}, bf16[2,2,16,1536]{3,2,1,0:T(8,128)(2,1)S(1)}, u32[]{:S(2)}, u32[]{:S(2)}) collective-permute-start(bf16[2,2,16,1536]{3,2,1,0:T(8,128)(2,1)S(1)} %collective-permute-done.3.refs_4_), channel_id=1, source_target_pairs={{0,7},{1,0},{2,1},{3,2},{4,3},{5,4},{6,5},{7,6},{8,15},{9,8},{10,9... | collective-permute-start | bytes 589832 | tf_op jit(solution)/shard_map/ppermute | solution.py:240
  41.2 0.1 pad_add_fusion.info
  41.2 0.0 collective-permute-done.6.refs_7_
  41.2 0.3 collective-permute-done.4.refs_5_
  41.6 2.8 %collective-permute-done.5.refs_6_ = bf16[2,2,16,1536]{3,2,1,0:T(8,128)(2,1)S(1)} collective-permute-done((bf16[2,2,16,1536]{3,2,1,0:T(8,128)(2,1)S(1)}, bf16[2,2,16,1536]{3,2,1,0:T(8,128)(2,1)S(1)}, u32[]{:S(2)}, u32[]{:S(2)}) %collective-permute-start.5) | collective-permute-done | bytes 196640 | tf_op jit(solution)/shard_map/ppermute | solution.py:240
  44.3 0.0 copy-start
  44.3 1.8 %shard_map.58 = (bf16[8,2,16,1536]{3,2,1,0:T(8,128)(2,1)}, bf16[8,16,1536]{2,1,0:T(8,128)(2,1)}, bf16[8,16,1536]{2,1,0:T(8,128)(2,1)}) custom-call(s32[3]{0:T(128)S(1)} %pad_add_fusion.info, bf16[2,2,16,1536]{3,2,1,0:T(8,128)(2,1)S(1)} %maximum_bitcast_fusion.refs_0_.own, bf16[2,2,16,1536]{3,2,1,0:T(8,128)(2,1)S(1)} %collective-permute-done.refs_1_, ...), custom_call_target="tpu_custom_call" | custom-call | tf_op jit(solution)/shard_map/pallas_call | solution.py:249
  46.2 1.9 %collective-permute-start.7 = (bf16[8,2,16,1536]{3,2,1,0:T(8,128)(2,1)}, bf16[8,2,16,1536]{3,2,1,0:T(8,128)(2,1)S(1)}, u32[]{:S(2)}, u32[]{:S(2)}) collective-permute-start(bf16[8,2,16,1536]{3,2,1,0:T(8,128)(2,1)} %get-tuple-element.10), channel_id=1, source_target_pairs={{0,16},{16,0},{1,17},{17,1},{2,18},{18,2},{3,19},{19,3},{4,20},{20... | collective-permute-start | bytes 2359304 | tf_op jit(solution)/shard_map/ppermute | solution.py:253
  48.1 4.7 %collective-permute-start.8 = (bf16[8,16,1536]{2,1,0:T(8,128)(2,1)}, bf16[8,16,1536]{2,1,0:T(8,128)(2,1)S(1)}, u32[]{:S(2)}, u32[]{:S(2)}) collective-permute-start(bf16[8,16,1536]{2,1,0:T(8,128)(2,1)} %get-tuple-element.11), channel_id=1, source_target_pairs={{0,496},{16,32},{32,16},{48,64},{64,48},{80,96},{96,80},{112,128},... | collective-permute-start | bytes 1179656 | tf_op jit(solution)/shard_map/ppermute | solution.py:251
  52.8 0.6 fusion.7.pick
  53.4 0.0 copy-done
  53.4 0.9 shard_map.61
  54.3 5.0 %all-to-all-start = ((bf16[8,32,512]{2,1,0:T(8,128)(2,1)}), bf16[8,32,512]{2,1,0:T(8,128)(2,1)S(1)}, u32[]{:S(2)}, u32[]{:S(2)}) async-start(bf16[8,32,512]{2,1,0:T(8,128)(2,1)} %shard_map.61), calls=%async_computation | async-start | bytes 524288 | tf_op jit(solution)/shard_map/all_to_all | solution.py:261
  59.3 0.6 shard_map.59
  59.9 7.7 %collective-permute-start.9 = (bf16[816,128]{1,0:T(8,128)(2,1)S(1)}, bf16[816,128]{1,0:T(8,128)(2,1)S(1)}, u32[]{:S(2)}, u32[]{:S(2)}) collective-permute-start(bf16[816,128]{1,0:T(8,128)(2,1)S(1)} %shard_map.59), channel_id=1, source_target_pairs={{0,8},{8,0},{1,9},{9,1},{2,10},{10,2},{3,11},{11,3},{4,12},{12,4},... | collective-permute-start | bytes 626696 | tf_op jit(solution)/shard_map/ppermute | solution.py:245
  67.6 1.9 %collective-permute-start.11 = (bf16[8,16,1536]{2,1,0:T(8,128)(2,1)}, bf16[8,16,1536]{2,1,0:T(8,128)(2,1)}, u32[]{:S(2)}, u32[]{:S(2)}) collective-permute-start(bf16[8,16,1536]{2,1,0:T(8,128)(2,1)} %get-tuple-element.14), channel_id=1, source_target_pairs={{0,496},{16,32},{32,16},{48,64},{64,48},{80,96},{96,80},{112,128},... | collective-permute-start | bytes 1179656 | tf_op jit(solution)/shard_map/ppermute | solution.py:252
  69.6 4.5 %collective-permute-done.9.refs_11_.refs_10_ = bf16[816,128]{1,0:T(8,128)(2,1)S(1)} collective-permute-done((bf16[816,128]{1,0:T(8,128)(2,1)S(1)}, bf16[816,128]{1,0:T(8,128)(2,1)S(1)}, u32[]{:S(2)}, u32[]{:S(2)}) %collective-permute-start.9) | collective-permute-done | bytes 208928 | tf_op jit(solution)/shard_map/ppermute | solution.py:245
  74.1 0.0 collective-permute-done.8.refs_9_
  74.1 0.0 collective-permute-done.7.refs_8_
  74.1 2.8 %shard_map.60 = (f32[16,3072]{1,0:T(8,128)S(1)}, f32[16,3072]{1,0:T(8,128)}) custom-call(s32[3]{0:T(128)S(1)} %pad_add_fusion.info, bf16[2,2,16,1536]{3,2,1,0:T(8,128)(2,1)S(1)} %maximum_bitcast_fusion.refs_0_.own, bf16[2,2,16,1536]{3,2,1,0:T(8,128)(2,1)S(1)} %collective-permute-done.refs_1_, bf16[2,2,16,1536]{3,2,1,0:T(8,128)(2,1)S(1)} %collective-permute-done.1.refs_2_, ...), custom_call_target="tpu_custom_call" | custom-call | tf_op jit(solution)/shard_map/pallas_call | solution.py:274
  76.9 0.0 copy-start.1
  76.9 0.7 copy-done.1
  77.5 7.0 %collective-permute-start.10 = (f32[16,3072]{1,0:T(8,128)}, f32[16,3072]{1,0:T(8,128)}, u32[]{:S(2)}, u32[]{:S(2)}) collective-permute-start(f32[16,3072]{1,0:T(8,128)} %get-tuple-element.13), channel_id=1, source_target_pairs={{0,8},{8,0},{1,9},{9,1},{2,10},{10,2},{3,11},{11,3},{4,12},{12,4},... | collective-permute-start | bytes 589832 | tf_op jit(solution)/shard_map/ppermute | solution.py:277
  84.6 0.0 all-to-all-done.refs_10_
  84.6 0.0 collective-permute-done.11.refs_9_
  84.6 4.0 %shard_map.62 = (f32[16,3072]{1,0:T(8,128)S(1)}, f32[16,3072]{1,0:T(8,128)}) custom-call(s32[3]{0:T(128)S(1)} %pad_add_fusion.info, bf16[2,2,16,1536]{3,2,1,0:T(8,128)(2,1)S(1)} %maximum_bitcast_fusion.refs_0_.own, bf16[2,2,16,1536]{3,2,1,0:T(8,128)(2,1)S(1)} %collective-permute-done.refs_1_, bf16[2,2,16,1536]{3,2,1,0:T(8,128)(2,1)S(1)} %collective-permute-done.1.refs_2_, ...), custom_call_target="tpu_custom_call" | custom-call | tf_op jit(solution)/shard_map/pallas_call | solution.py:278
  88.7 2.7 %collective-permute-start.12 = (f32[16,3072]{1,0:T(8,128)}, f32[16,3072]{1,0:T(8,128)S(1)}, u32[]{:S(2)}, u32[]{:S(2)}) collective-permute-start(f32[16,3072]{1,0:T(8,128)} %get-tuple-element.16), channel_id=1, source_target_pairs={{0,8},{8,0},{1,9},{9,1},{2,10},{10,2},{3,11},{11,3},{4,12},{12,4},... | collective-permute-start | bytes 589832 | tf_op jit(solution)/shard_map/ppermute | solution.py:281
  91.3 3.7 %shard_map.63 = f32[8,4,8,432]{3,2,1,0:T(8,128)} custom-call(s32[3]{0:T(128)S(1)} %pad_add_fusion.info, bf16[2,2,16,1536]{3,2,1,0:T(8,128)(2,1)S(1)} %maximum_bitcast_fusion.refs_0_.own, bf16[2,2,16,1536]{3,2,1,0:T(8,128)(2,1)S(1)} %collective-permute-done.refs_1_, bf16[2,2,16,1536]{3,2,1,0:T(8,128)(2,1)S(1)} %collective-permute-done.1.refs_2_, ...), custom_call_target="tpu_custom_call" | custom-call | tf_op jit(solution)/shard_map/pallas_call | solution.py:267
  95.1 0.0 copy-start.2
  95.1 6.1 %all-to-all-start.1 = ((f32[8,4,8,432]{3,2,1,0:T(8,128)}), f32[8,4,8,432]{3,2,1,0:T(8,128)S(1)}, u32[]{:S(2)}, u32[]{:S(2)}) async-start(f32[8,4,8,432]{3,2,1,0:T(8,128)} %shard_map.63), calls=%async_computation.1 | async-start | bytes 1048576 | tf_op jit(solution)/shard_map/all_to_all | solution.py:273
  101.2 0.0 collective-permute-done.10
  101.2 0.0 copy-done.2
  101.2 0.9 add_convert_fusion.1
  102.2 9.3 %all-to-all-done.1.got = f32[8,4,8,432]{3,2,1,0:T(8,128)S(1)} async-done(((f32[8,4,8,432]{3,2,1,0:T(8,128)}), f32[8,4,8,432]{3,2,1,0:T(8,128)S(1)}, u32[]{:S(2)}, u32[]{:S(2)}) %all-to-all-start.1) | async-done | bytes 442400 | tf_op jit(solution)/shard_map/all_to_all | solution.py:273
  111.5 1.2 shard_map.64
  112.7 7.3 %all-to-all-start.2 = ((f32[8,8,432]{2,1,0:T(8,128)}), f32[8,8,432]{2,1,0:T(8,128)S(1)}, u32[]{:S(2)}, u32[]{:S(2)}) async-start(f32[8,8,432]{2,1,0:T(8,128)} %shard_map.64), calls=%async_computation.2 | async-start | bytes 262144 | tf_op jit(solution)/shard_map/all_to_all | solution.py:284
  120.1 0.0 collective-permute-done.12
  120.1 0.7 reshape.20
  120.8 0.7 reshape.21
  121.5 6.0 %all-to-all-done.2 = f32[8,8,432]{2,1,0:T(8,128)S(1)} async-done(((f32[8,8,432]{2,1,0:T(8,128)}), f32[8,8,432]{2,1,0:T(8,128)S(1)}, u32[]{:S(2)}, u32[]{:S(2)}) %all-to-all-start.2) | async-done | bytes 110624 | tf_op jit(solution)/shard_map/all_to_all | solution.py:284
  127.5 0.1 mul.25
  127.6 0.7 copy.10
  (9 shorter events, 0.1 us)
Async XLA Ops:
  1.6 15.8 %collective-permute-start = (bf16[2,2,16,1536]{3,2,1,0:T(8,128)(2,1)S(1)}, bf16[2,2,16,1536]{3,2,1,0:T(8,128)(2,1)S(1)}, u32[]{:S(2)}, u32[]{:S(2)}) collective-permute-start(bf16[2,2,16,1536]{3,2,1,0:T(8,128)(2,1)S(1)} %maximum_bitcast_fusion.refs_0_.own), channel_id=1, source_target_pairs={{0,1},{1,2},{2,3},{3,4},{4,5},{5,6},{6,7},{7,0},{8,9},{9,10},{10,1... | collective-permute-start | bytes 589832 | tf_op jit(solution)/shard_map/ppermute | solution.py:239
  5.9 13.5 %collective-permute-start.1 = (bf16[2,2,16,1536]{3,2,1,0:T(8,128)(2,1)S(1)}, bf16[2,2,16,1536]{3,2,1,0:T(8,128)(2,1)S(1)}, u32[]{:S(2)}, u32[]{:S(2)}) collective-permute-start(bf16[2,2,16,1536]{3,2,1,0:T(8,128)(2,1)S(1)} %maximum_bitcast_fusion.refs_0_.own), channel_id=1, source_target_pairs={{0,7},{1,0},{2,1},{3,2},{4,3},{5,4},{6,5},{7,6},{8,15},{9,8},{10,9... | collective-permute-start | bytes 589832 | tf_op jit(solution)/shard_map/ppermute | solution.py:240
  17.5 11.9 %collective-permute-start.2 = (bf16[2,2,16,1536]{3,2,1,0:T(8,128)(2,1)S(1)}, bf16[2,2,16,1536]{3,2,1,0:T(8,128)(2,1)S(1)}, u32[]{:S(2)}, u32[]{:S(2)}) collective-permute-start(bf16[2,2,16,1536]{3,2,1,0:T(8,128)(2,1)S(1)} %collective-permute-done.refs_1_), channel_id=1, source_target_pairs={{0,1},{1,2},{2,3},{3,4},{4,5},{5,6},{6,7},{7,0},{8,9},{9,10},{10,1... | collective-permute-start | bytes 589832 | tf_op jit(solution)/shard_map/ppermute | solution.py:239
  19.4 16.0 %collective-permute-start.3 = (bf16[2,2,16,1536]{3,2,1,0:T(8,128)(2,1)S(1)}, bf16[2,2,16,1536]{3,2,1,0:T(8,128)(2,1)S(1)}, u32[]{:S(2)}, u32[]{:S(2)}) collective-permute-start(bf16[2,2,16,1536]{3,2,1,0:T(8,128)(2,1)S(1)} %collective-permute-done.1.refs_2_), channel_id=1, source_target_pairs={{0,7},{1,0},{2,1},{3,2},{4,3},{5,4},{6,5},{7,6},{8,15},{9,8},{10,9... | collective-permute-start | bytes 589832 | tf_op jit(solution)/shard_map/ppermute | solution.py:240
  24.5 16.7 %collective-permute-start.6 = (bf16[2,2,16,1536]{3,2,1,0:T(8,128)(2,1)S(1)}, bf16[2,2,16,1536]{3,2,1,0:T(8,128)(2,1)S(1)}, u32[]{:S(2)}, u32[]{:S(2)}) collective-permute-start(bf16[2,2,16,1536]{3,2,1,0:T(8,128)(2,1)S(1)} %maximum_bitcast_fusion.refs_0_.own), channel_id=1, source_target_pairs={{0,4},{1,5},{2,6},{3,7},{4,0},{5,1},{6,2},{7,3},{8,12},{9,13},{10,... | collective-permute-start | bytes 589832 | tf_op jit(solution)/shard_map/ppermute | solution.py:242
  29.4 12.2 %collective-permute-start.4 = (bf16[2,2,16,1536]{3,2,1,0:T(8,128)(2,1)S(1)}, bf16[2,2,16,1536]{3,2,1,0:T(8,128)(2,1)S(1)}, u32[]{:S(2)}, u32[]{:S(2)}) collective-permute-start(bf16[2,2,16,1536]{3,2,1,0:T(8,128)(2,1)S(1)} %collective-permute-done.2.refs_3_), channel_id=1, source_target_pairs={{0,1},{1,2},{2,3},{3,4},{4,5},{5,6},{6,7},{7,0},{8,9},{9,10},{10,1... | collective-permute-start | bytes 589832 | tf_op jit(solution)/shard_map/ppermute | solution.py:239
  35.4 8.9 %collective-permute-start.5 = (bf16[2,2,16,1536]{3,2,1,0:T(8,128)(2,1)S(1)}, bf16[2,2,16,1536]{3,2,1,0:T(8,128)(2,1)S(1)}, u32[]{:S(2)}, u32[]{:S(2)}) collective-permute-start(bf16[2,2,16,1536]{3,2,1,0:T(8,128)(2,1)S(1)} %collective-permute-done.3.refs_4_), channel_id=1, source_target_pairs={{0,7},{1,0},{2,1},{3,2},{4,3},{5,4},{6,5},{7,6},{8,15},{9,8},{10,9... | collective-permute-start | bytes 589832 | tf_op jit(solution)/shard_map/ppermute | solution.py:240
  44.3 9.1 %copy-start = (bf16[27,16,256]{2,1,0:T(8,128)(2,1)S(1)}, bf16[27,16,256]{2,1,0:T(8,128)(2,1)}, u32[]{:S(2)}) copy-start(bf16[27,16,256]{2,1,0:T(8,128)(2,1)} %param.4) | copy-start | bytes 663556
  46.2 27.9 %collective-permute-start.7 = (bf16[8,2,16,1536]{3,2,1,0:T(8,128)(2,1)}, bf16[8,2,16,1536]{3,2,1,0:T(8,128)(2,1)S(1)}, u32[]{:S(2)}, u32[]{:S(2)}) collective-permute-start(bf16[8,2,16,1536]{3,2,1,0:T(8,128)(2,1)} %get-tuple-element.10), channel_id=1, source_target_pairs={{0,16},{16,0},{1,17},{17,1},{2,18},{18,2},{3,19},{19,3},{4,20},{20... | collective-permute-start | bytes 2359304 | tf_op jit(solution)/shard_map/ppermute | solution.py:253
  48.1 26.0 %collective-permute-start.8 = (bf16[8,16,1536]{2,1,0:T(8,128)(2,1)}, bf16[8,16,1536]{2,1,0:T(8,128)(2,1)S(1)}, u32[]{:S(2)}, u32[]{:S(2)}) collective-permute-start(bf16[8,16,1536]{2,1,0:T(8,128)(2,1)} %get-tuple-element.11), channel_id=1, source_target_pairs={{0,496},{16,32},{32,16},{48,64},{64,48},{80,96},{96,80},{112,128},... | collective-permute-start | bytes 1179656 | tf_op jit(solution)/shard_map/ppermute | solution.py:251
  54.3 30.2 %all-to-all-start = ((bf16[8,32,512]{2,1,0:T(8,128)(2,1)}), bf16[8,32,512]{2,1,0:T(8,128)(2,1)S(1)}, u32[]{:S(2)}, u32[]{:S(2)}) async-start(bf16[8,32,512]{2,1,0:T(8,128)(2,1)} %shard_map.61), calls=%async_computation | async-start | bytes 524288 | tf_op jit(solution)/shard_map/all_to_all | solution.py:261
  59.9 14.2 %collective-permute-start.9 = (bf16[816,128]{1,0:T(8,128)(2,1)S(1)}, bf16[816,128]{1,0:T(8,128)(2,1)S(1)}, u32[]{:S(2)}, u32[]{:S(2)}) collective-permute-start(bf16[816,128]{1,0:T(8,128)(2,1)S(1)} %shard_map.59), channel_id=1, source_target_pairs={{0,8},{8,0},{1,9},{9,1},{2,10},{10,2},{3,11},{11,3},{4,12},{12,4},... | collective-permute-start | bytes 626696 | tf_op jit(solution)/shard_map/ppermute | solution.py:245
  67.6 17.0 %collective-permute-start.11 = (bf16[8,16,1536]{2,1,0:T(8,128)(2,1)}, bf16[8,16,1536]{2,1,0:T(8,128)(2,1)}, u32[]{:S(2)}, u32[]{:S(2)}) collective-permute-start(bf16[8,16,1536]{2,1,0:T(8,128)(2,1)} %get-tuple-element.14), channel_id=1, source_target_pairs={{0,496},{16,32},{32,16},{48,64},{64,48},{80,96},{96,80},{112,128},... | collective-permute-start | bytes 1179656 | tf_op jit(solution)/shard_map/ppermute | solution.py:252
  76.9 0.7 copy-start.1
  77.5 23.7 %collective-permute-start.10 = (f32[16,3072]{1,0:T(8,128)}, f32[16,3072]{1,0:T(8,128)}, u32[]{:S(2)}, u32[]{:S(2)}) collective-permute-start(f32[16,3072]{1,0:T(8,128)} %get-tuple-element.13), channel_id=1, source_target_pairs={{0,8},{8,0},{1,9},{9,1},{2,10},{10,2},{3,11},{11,3},{4,12},{12,4},... | collective-permute-start | bytes 589832 | tf_op jit(solution)/shard_map/ppermute | solution.py:277
  88.7 31.4 %collective-permute-start.12 = (f32[16,3072]{1,0:T(8,128)}, f32[16,3072]{1,0:T(8,128)S(1)}, u32[]{:S(2)}, u32[]{:S(2)}) collective-permute-start(f32[16,3072]{1,0:T(8,128)} %get-tuple-element.16), channel_id=1, source_target_pairs={{0,8},{8,0},{1,9},{9,1},{2,10},{10,2},{3,11},{11,3},{4,12},{12,4},... | collective-permute-start | bytes 589832 | tf_op jit(solution)/shard_map/ppermute | solution.py:281
  95.1 6.1 %copy-start.2 = (f32[16,3072]{1,0:T(8,128)S(1)}, f32[16,3072]{1,0:T(8,128)}, u32[]{:S(2)}) copy-start(f32[16,3072]{1,0:T(8,128)} %copy-done.1) | copy-start | bytes 589828
  95.1 16.4 %all-to-all-start.1 = ((f32[8,4,8,432]{3,2,1,0:T(8,128)}), f32[8,4,8,432]{3,2,1,0:T(8,128)S(1)}, u32[]{:S(2)}, u32[]{:S(2)}) async-start(f32[8,4,8,432]{3,2,1,0:T(8,128)} %shard_map.63), calls=%async_computation.1 | async-start | bytes 1048576 | tf_op jit(solution)/shard_map/all_to_all | solution.py:273
  112.7 14.8 %all-to-all-start.2 = ((f32[8,8,432]{2,1,0:T(8,128)}), f32[8,8,432]{2,1,0:T(8,128)S(1)}, u32[]{:S(2)}, u32[]{:S(2)}) async-start(f32[8,8,432]{2,1,0:T(8,128)} %shard_map.64), calls=%async_computation.2 | async-start | bytes 262144 | tf_op jit(solution)/shard_map/all_to_all | solution.py:284

commit v4 on v3

--- a/solution.py
+++ b/solution.py
@@ -151,9 +151,13 @@
     conv(field, weights, prod, out_own, out_far, -1)
 
 
-def chunks_kernel(pick, flat, out):
+def chunks_kernel(info, flat, out):
+    row = lax.broadcasted_iota(jnp.int32, (256, 256), 0)
+    col = lax.broadcasted_iota(jnp.int32, (256, 256), 1)
+    half = (info[2] + (row >> 4)) & 1
+    pick = (col == half * 128 + (row >> 5) * 16 + (row & 15)).astype(F32).astype(BF)
     v = lax.dot_general(
-        pick[...], flat[...], (((1,), (1,)), ((), ())), preferred_element_type=F32
+        pick, flat[...], (((1,), (1,)), ((), ())), preferred_element_type=F32
     ).astype(BF)
     for k in range(8):
         out[k, :, pl.ds(0, 432)] = v[32 * k : 32 * k + 32]
@@ -220,7 +224,7 @@
         in_specs=in_specs,
         out_specs=jax.tree.map(lambda _: VM, outs),
         scratch_shapes=scratch,
-        compiler_params=pltpu.CompilerParams(vmem_limit_bytes=48 * 1024 * 1024),
+        compiler_params=pltpu.CompilerParams(vmem_limit_bytes=24 * 1024 * 1024),
     )
 
 
@@ -252,12 +256,7 @@
     outer_g = lax.ppermute(outer_g, SLAB, outer_pairs)
     inner = lax.ppermute(inner, "core", swap)
 
-    row = lax.broadcasted_iota(jnp.int32, (256, 256), 0)
-    col = lax.broadcasted_iota(jnp.int32, (256, 256), 1)
-    zz, m, i = row // 32, (row // 16) % 2, row % 16
-    wanted = ((yh + m) % 2) * 128 + zz * 16 + i
-    pick = (col == wanted).astype(BF)
-    chunks = call(chunks_kernel, shape((8, 32, 512), BF), [VM, VM])(pick, flat)
+    chunks = call(chunks_kernel, shape((8, 32, 512), BF), [SM, VM])(info, flat)
     turned = lax.all_to_all(chunks, "z", 0, 0, tiled=True)
 
     piece = shape((16, 2 * PLANE), F32)

time: 129 us -> 129 us (level)
  transfers between devices with their start and end apart: 16 -> 16, of which waited for: 7 -> 7; matrix products, arithmetic and copies ran while one was open for 2% -> 2% of each run, Pallas kernels for 10% -> 11%
where the time goes in v4:
time: 129 us; the launch traced here: 128 us
  starting transfers between devices  76.7 us (59%)
  waiting for transfers between devices  30.1 us (23%)
  Pallas kernels  15.7 us (12%)
  local copies, waits for them, and re-layouts  3.85 us (3%)
    ppermute x3, starting transfers between devices, run(): b = lax.ppermute(b, 'z', down)  19.5 us
    all_to_all x1, waiting for transfers between devices, run(): got = lax.all_to_all(filt, ('x', 'core'), 0, 0, tiled=True)  9.35 us
    ppermute x3, starting transfers between devices, run(): a = lax.ppermute(a, 'z', up)  8.11 us
    ppermute x1, starting transfers between devices, run(): packed = lax.ppermute(packed, 'yh', swap)  7.73 us
    all_to_all x1, starting transfers between devices, run(): got = lax.all_to_all(got, ('yl1', 'yl0', 'yh'), 0, 0, tiled=True)  7.32 us
    ppermute x1, starting transfers between devices, run(): feat_in = lax.ppermute(feat_far, 'yh', swap)  7.05 us
    ppermute x3, waiting for transfers between devices, run(): b = lax.ppermute(b, 'z', down)  6.9 us
    all_to_all x1, starting transfers between devices, run(): got = lax.all_to_all(filt, ('x', 'core'), 0, 0, tiled=True)  6.11 us
  transfers between devices with their start and end apart: 16, of which 7 were waited for; matrix products, arithmetic and copies ran while one was open for 2% of the time, Pallas kernels for 11%

profile of v4, /device:TPU:8, one launch (start us, length us, event | category | flops | bytes accessed | tf_op | source)
XLA Modules:
  0.0 128.3 jit_solution(13014368065613212170)
XLA Ops:
  0.6 1.0 copy_bitcast_fusion
  1.6 4.3 %collective-permute-start = (bf16[2,2,16,1536]{3,2,1,0:T(8,128)(2,1)S(1)}, bf16[2,2,16,1536]{3,2,1,0:T(8,128)(2,1)S(1)}, u32[]{:S(2)}, u32[]{:S(2)}) collective-permute-start(bf16[2,2,16,1536]{3,2,1,0:T(8,128)(2,1)S(1)} %maximum_bitcast_fusion.refs_0_.own), channel_id=1, source_target_pairs={{0,1},{1,2},{2,3},{3,4},{4,5},{5,6},{6,7},{7,0},{8,9},{9,10},{10,1... | collective-permute-start | bytes 589832 | tf_op jit(solution)/shard_map/ppermute | solution.py:243
  5.9 8.6 %collective-permute-start.1 = (bf16[2,2,16,1536]{3,2,1,0:T(8,128)(2,1)S(1)}, bf16[2,2,16,1536]{3,2,1,0:T(8,128)(2,1)S(1)}, u32[]{:S(2)}, u32[]{:S(2)}) collective-permute-start(bf16[2,2,16,1536]{3,2,1,0:T(8,128)(2,1)S(1)} %maximum_bitcast_fusion.refs_0_.own), channel_id=1, source_target_pairs={{0,7},{1,0},{2,1},{3,2},{4,3},{5,4},{6,5},{7,6},{8,15},{9,8},{10,9... | collective-permute-start | bytes 589832 | tf_op jit(solution)/shard_map/ppermute | solution.py:244
  14.5 3.0 %collective-permute-done.refs_1_ = bf16[2,2,16,1536]{3,2,1,0:T(8,128)(2,1)S(1)} collective-permute-done((bf16[2,2,16,1536]{3,2,1,0:T(8,128)(2,1)S(1)}, bf16[2,2,16,1536]{3,2,1,0:T(8,128)(2,1)S(1)}, u32[]{:S(2)}, u32[]{:S(2)}) %collective-permute-start) | collective-permute-done | bytes 196640 | tf_op jit(solution)/shard_map/ppermute | solution.py:243
  17.5 1.9 %collective-permute-start.2 = (bf16[2,2,16,1536]{3,2,1,0:T(8,128)(2,1)S(1)}, bf16[2,2,16,1536]{3,2,1,0:T(8,128)(2,1)S(1)}, u32[]{:S(2)}, u32[]{:S(2)}) collective-permute-start(bf16[2,2,16,1536]{3,2,1,0:T(8,128)(2,1)S(1)} %collective-permute-done.refs_1_), channel_id=1, source_target_pairs={{0,1},{1,2},{2,3},{3,4},{4,5},{5,6},{6,7},{7,0},{8,9},{9,10},{10,1... | collective-permute-start | bytes 589832 | tf_op jit(solution)/shard_map/ppermute | solution.py:243
  19.4 0.0 collective-permute-done.1.refs_2_
  19.4 5.1 %collective-permute-start.3 = (bf16[2,2,16,1536]{3,2,1,0:T(8,128)(2,1)S(1)}, bf16[2,2,16,1536]{3,2,1,0:T(8,128)(2,1)S(1)}, u32[]{:S(2)}, u32[]{:S(2)}) collective-permute-start(bf16[2,2,16,1536]{3,2,1,0:T(8,128)(2,1)S(1)} %collective-permute-done.1.refs_2_), channel_id=1, source_target_pairs={{0,7},{1,0},{2,1},{3,2},{4,3},{5,4},{6,5},{7,6},{8,15},{9,8},{10,9... | collective-permute-start | bytes 589832 | tf_op jit(solution)/shard_map/ppermute | solution.py:244
  24.5 4.8 %collective-permute-start.6 = (bf16[2,2,16,1536]{3,2,1,0:T(8,128)(2,1)S(1)}, bf16[2,2,16,1536]{3,2,1,0:T(8,128)(2,1)S(1)}, u32[]{:S(2)}, u32[]{:S(2)}) collective-permute-start(bf16[2,2,16,1536]{3,2,1,0:T(8,128)(2,1)S(1)} %maximum_bitcast_fusion.refs_0_.own), channel_id=1, source_target_pairs={{0,4},{1,5},{2,6},{3,7},{4,0},{5,1},{6,2},{7,3},{8,12},{9,13},{10,... | collective-permute-start | bytes 589832 | tf_op jit(solution)/shard_map/ppermute | solution.py:246
  29.4 0.0 collective-permute-done.2.refs_3_
  29.4 1.9 %collective-permute-start.4 = (bf16[2,2,16,1536]{3,2,1,0:T(8,128)(2,1)S(1)}, bf16[2,2,16,1536]{3,2,1,0:T(8,128)(2,1)S(1)}, u32[]{:S(2)}, u32[]{:S(2)}) collective-permute-start(bf16[2,2,16,1536]{3,2,1,0:T(8,128)(2,1)S(1)} %collective-permute-done.2.refs_3_), channel_id=1, source_target_pairs={{0,1},{1,2},{2,3},{3,4},{4,5},{5,6},{6,7},{7,0},{8,9},{9,10},{10,1... | collective-permute-start | bytes 589832 | tf_op jit(solution)/shard_map/ppermute | solution.py:243
  31.3 4.1 %collective-permute-done.3.refs_4_ = bf16[2,2,16,1536]{3,2,1,0:T(8,128)(2,1)S(1)} collective-permute-done((bf16[2,2,16,1536]{3,2,1,0:T(8,128)(2,1)S(1)}, bf16[2,2,16,1536]{3,2,1,0:T(8,128)(2,1)S(1)}, u32[]{:S(2)}, u32[]{:S(2)}) %collective-permute-start.3) | collective-permute-done | bytes 196640 | tf_op jit(solution)/shard_map/ppermute | solution.py:244
  35.4 5.7 %collective-permute-start.5 = (bf16[2,2,16,1536]{3,2,1,0:T(8,128)(2,1)S(1)}, bf16[2,2,16,1536]{3,2,1,0:T(8,128)(2,1)S(1)}, u32[]{:S(2)}, u32[]{:S(2)}) collective-permute-start(bf16[2,2,16,1536]{3,2,1,0:T(8,128)(2,1)S(1)} %collective-permute-done.3.refs_4_), channel_id=1, source_target_pairs={{0,7},{1,0},{2,1},{3,2},{4,3},{5,4},{6,5},{7,6},{8,15},{9,8},{10,9... | collective-permute-start | bytes 589832 | tf_op jit(solution)/shard_map/ppermute | solution.py:244
  41.2 0.1 pad_add_fusion.info
  41.2 0.0 copy-start
  41.2 0.0 collective-permute-done.6.refs_7_
  41.2 0.3 collective-permute-done.4.refs_5_
  41.5 2.8 %collective-permute-done.5.refs_6_ = bf16[2,2,16,1536]{3,2,1,0:T(8,128)(2,1)S(1)} collective-permute-done((bf16[2,2,16,1536]{3,2,1,0:T(8,128)(2,1)S(1)}, bf16[2,2,16,1536]{3,2,1,0:T(8,128)(2,1)S(1)}, u32[]{:S(2)}, u32[]{:S(2)}) %collective-permute-start.5) | collective-permute-done | bytes 196640 | tf_op jit(solution)/shard_map/ppermute | solution.py:244
  44.3 1.8 %shard_map.58 = (bf16[8,2,16,1536]{3,2,1,0:T(8,128)(2,1)}, bf16[8,16,1536]{2,1,0:T(8,128)(2,1)}, bf16[8,16,1536]{2,1,0:T(8,128)(2,1)}) custom-call(s32[3]{0:T(128)S(1)} %pad_add_fusion.info, bf16[2,2,16,1536]{3,2,1,0:T(8,128)(2,1)S(1)} %maximum_bitcast_fusion.refs_0_.own, bf16[2,2,16,1536]{3,2,1,0:T(8,128)(2,1)S(1)} %collective-permute-done.refs_1_, ...), custom_call_target="tpu_custom_call" | custom-call | tf_op jit(solution)/shard_map/pallas_call | solution.py:253
  46.1 1.9 %collective-permute-start.7 = (bf16[8,2,16,1536]{3,2,1,0:T(8,128)(2,1)}, bf16[8,2,16,1536]{3,2,1,0:T(8,128)(2,1)S(1)}, u32[]{:S(2)}, u32[]{:S(2)}) collective-permute-start(bf16[8,2,16,1536]{3,2,1,0:T(8,128)(2,1)} %get-tuple-element.10), channel_id=1, source_target_pairs={{0,16},{16,0},{1,17},{17,1},{2,18},{18,2},{3,19},{19,3},{4,20},{20... | collective-permute-start | bytes 2359304 | tf_op jit(solution)/shard_map/ppermute | solution.py:257
  48.1 4.7 %collective-permute-start.8 = (bf16[8,16,1536]{2,1,0:T(8,128)(2,1)}, bf16[8,16,1536]{2,1,0:T(8,128)(2,1)S(1)}, u32[]{:S(2)}, u32[]{:S(2)}) collective-permute-start(bf16[8,16,1536]{2,1,0:T(8,128)(2,1)} %get-tuple-element.11), channel_id=1, source_target_pairs={{0,496},{16,32},{32,16},{48,64},{64,48},{80,96},{96,80},{112,128},... | collective-permute-start | bytes 1179656 | tf_op jit(solution)/shard_map/ppermute | solution.py:255
  52.7 0.0 copy-done
  52.7 1.5 %shard_map.61 = bf16[8,32,512]{2,1,0:T(8,128)(2,1)} custom-call(s32[3]{0:T(128)S(1)} %pad_add_fusion.info, bf16[432,256]{1,0:T(8,128)(2,1)S(1)} %bitcast.11), custom_call_target="tpu_custom_call" | custom-call | tf_op jit(solution)/shard_map/pallas_call | solution.py:259
  54.2 5.0 %all-to-all-start = ((bf16[8,32,512]{2,1,0:T(8,128)(2,1)}), bf16[8,32,512]{2,1,0:T(8,128)(2,1)S(1)}, u32[]{:S(2)}, u32[]{:S(2)}) async-start(bf16[8,32,512]{2,1,0:T(8,128)(2,1)} %shard_map.61), calls=%async_computation | async-start | bytes 524288 | tf_op jit(solution)/shard_map/all_to_all | solution.py:260
  59.2 0.6 shard_map.59
  59.8 7.7 %collective-permute-start.9 = (bf16[816,128]{1,0:T(8,128)(2,1)S(1)}, bf16[816,128]{1,0:T(8,128)(2,1)S(1)}, u32[]{:S(2)}, u32[]{:S(2)}) collective-permute-start(bf16[816,128]{1,0:T(8,128)(2,1)S(1)} %shard_map.59), channel_id=1, source_target_pairs={{0,8},{8,0},{1,9},{9,1},{2,10},{10,2},{3,11},{11,3},{4,12},{12,4},... | collective-permute-start | bytes 626696 | tf_op jit(solution)/shard_map/ppermute | solution.py:249
  67.5 1.9 %collective-permute-start.11 = (bf16[8,16,1536]{2,1,0:T(8,128)(2,1)}, bf16[8,16,1536]{2,1,0:T(8,128)(2,1)}, u32[]{:S(2)}, u32[]{:S(2)}) collective-permute-start(bf16[8,16,1536]{2,1,0:T(8,128)(2,1)} %get-tuple-element.14), channel_id=1, source_target_pairs={{0,496},{16,32},{32,16},{48,64},{64,48},{80,96},{96,80},{112,128},... | collective-permute-start | bytes 1179656 | tf_op jit(solution)/shard_map/ppermute | solution.py:256
  69.5 4.5 %collective-permute-done.9.refs_11_.refs_10_ = bf16[816,128]{1,0:T(8,128)(2,1)S(1)} collective-permute-done((bf16[816,128]{1,0:T(8,128)(2,1)S(1)}, bf16[816,128]{1,0:T(8,128)(2,1)S(1)}, u32[]{:S(2)}, u32[]{:S(2)}) %collective-permute-start.9) | collective-permute-done | bytes 208928 | tf_op jit(solution)/shard_map/ppermute | solution.py:249
  73.9 0.0 collective-permute-done.8.refs_9_
  74.0 0.0 collective-permute-done.7.refs_8_
  74.0 2.8 %shard_map.60 = (f32[16,3072]{1,0:T(8,128)S(1)}, f32[16,3072]{1,0:T(8,128)}) custom-call(s32[3]{0:T(128)S(1)} %pad_add_fusion.info, bf16[2,2,16,1536]{3,2,1,0:T(8,128)(2,1)S(1)} %maximum_bitcast_fusion.refs_0_.own, bf16[2,2,16,1536]{3,2,1,0:T(8,128)(2,1)S(1)} %collective-permute-done.refs_1_, bf16[2,2,16,1536]{3,2,1,0:T(8,128)(2,1)S(1)} %collective-permute-done.1.refs_2_, ...), custom_call_target="tpu_custom_call" | custom-call | tf_op jit(solution)/shard_map/pallas_call | solution.py:273
  76.7 0.0 copy-start.1
  76.7 0.7 copy-done.1
  77.4 7.0 %collective-permute-start.10 = (f32[16,3072]{1,0:T(8,128)}, f32[16,3072]{1,0:T(8,128)}, u32[]{:S(2)}, u32[]{:S(2)}) collective-permute-start(f32[16,3072]{1,0:T(8,128)} %get-tuple-element.13), channel_id=1, source_target_pairs={{0,8},{8,0},{1,9},{9,1},{2,10},{10,2},{3,11},{11,3},{4,12},{12,4},... | collective-permute-start | bytes 589832 | tf_op jit(solution)/shard_map/ppermute | solution.py:276
  84.5 0.0 all-to-all-done.refs_10_
  84.5 0.0 collective-permute-done.11.refs_9_
  84.5 4.0 %shard_map.62 = (f32[16,3072]{1,0:T(8,128)S(1)}, f32[16,3072]{1,0:T(8,128)}) custom-call(s32[3]{0:T(128)S(1)} %pad_add_fusion.info, bf16[2,2,16,1536]{3,2,1,0:T(8,128)(2,1)S(1)} %maximum_bitcast_fusion.refs_0_.own, bf16[2,2,16,1536]{3,2,1,0:T(8,128)(2,1)S(1)} %collective-permute-done.refs_1_, bf16[2,2,16,1536]{3,2,1,0:T(8,128)(2,1)S(1)} %collective-permute-done.1.refs_2_, ...), custom_call_target="tpu_custom_call" | custom-call | tf_op jit(solution)/shard_map/pallas_call | solution.py:277
  88.5 2.7 %collective-permute-start.12 = (f32[16,3072]{1,0:T(8,128)}, f32[16,3072]{1,0:T(8,128)S(1)}, u32[]{:S(2)}, u32[]{:S(2)}) collective-permute-start(f32[16,3072]{1,0:T(8,128)} %get-tuple-element.16), channel_id=1, source_target_pairs={{0,8},{8,0},{1,9},{9,1},{2,10},{10,2},{3,11},{11,3},{4,12},{12,4},... | collective-permute-start | bytes 589832 | tf_op jit(solution)/shard_map/ppermute | solution.py:280
  91.2 3.7 %shard_map.63 = f32[8,4,8,432]{3,2,1,0:T(8,128)} custom-call(s32[3]{0:T(128)S(1)} %pad_add_fusion.info, bf16[2,2,16,1536]{3,2,1,0:T(8,128)(2,1)S(1)} %maximum_bitcast_fusion.refs_0_.own, bf16[2,2,16,1536]{3,2,1,0:T(8,128)(2,1)S(1)} %collective-permute-done.refs_1_, bf16[2,2,16,1536]{3,2,1,0:T(8,128)(2,1)S(1)} %collective-permute-done.1.refs_2_, ...), custom_call_target="tpu_custom_call" | custom-call | tf_op jit(solution)/shard_map/pallas_call | solution.py:266
  95.0 0.0 copy-start.2
  95.0 6.1 %all-to-all-start.1 = ((f32[8,4,8,432]{3,2,1,0:T(8,128)}), f32[8,4,8,432]{3,2,1,0:T(8,128)S(1)}, u32[]{:S(2)}, u32[]{:S(2)}) async-start(f32[8,4,8,432]{3,2,1,0:T(8,128)} %shard_map.63), calls=%async_computation.1 | async-start | bytes 1048576 | tf_op jit(solution)/shard_map/all_to_all | solution.py:272
  101.1 0.0 collective-permute-done.10
  101.1 0.0 copy-done.2
  101.1 0.9 add_convert_fusion.1
  102.0 9.3 %all-to-all-done.1.got = f32[8,4,8,432]{3,2,1,0:T(8,128)S(1)} async-done(((f32[8,4,8,432]{3,2,1,0:T(8,128)}), f32[8,4,8,432]{3,2,1,0:T(8,128)S(1)}, u32[]{:S(2)}, u32[]{:S(2)}) %all-to-all-start.1) | async-done | bytes 442400 | tf_op jit(solution)/shard_map/all_to_all | solution.py:272
  111.4 1.2 shard_map.64
  112.6 7.3 %all-to-all-start.2 = ((f32[8,8,432]{2,1,0:T(8,128)}), f32[8,8,432]{2,1,0:T(8,128)S(1)}, u32[]{:S(2)}, u32[]{:S(2)}) async-start(f32[8,8,432]{2,1,0:T(8,128)} %shard_map.64), calls=%async_computation.2 | async-start | bytes 262144 | tf_op jit(solution)/shard_map/all_to_all | solution.py:283
  119.9 0.0 collective-permute-done.12
  120.0 0.7 reshape.20
  120.7 0.7 reshape.21
  121.3 6.0 %all-to-all-done.2 = f32[8,8,432]{2,1,0:T(8,128)S(1)} async-done(((f32[8,8,432]{2,1,0:T(8,128)}), f32[8,8,432]{2,1,0:T(8,128)S(1)}, u32[]{:S(2)}, u32[]{:S(2)}) %all-to-all-start.2) | async-done | bytes 110624 | tf_op jit(solution)/shard_map/all_to_all | solution.py:283
  127.4 0.1 mul.12
  127.5 0.7 copy.10
  (4 shorter events, 0.1 us)
Async XLA Ops:
  1.6 15.8 %collective-permute-start = (bf16[2,2,16,1536]{3,2,1,0:T(8,128)(2,1)S(1)}, bf16[2,2,16,1536]{3,2,1,0:T(8,128)(2,1)S(1)}, u32[]{:S(2)}, u32[]{:S(2)}) collective-permute-start(bf16[2,2,16,1536]{3,2,1,0:T(8,128)(2,1)S(1)} %maximum_bitcast_fusion.refs_0_.own), channel_id=1, source_target_pairs={{0,1},{1,2},{2,3},{3,4},{4,5},{5,6},{6,7},{7,0},{8,9},{9,10},{10,1... | collective-permute-start | bytes 589832 | tf_op jit(solution)/shard_map/ppermute | solution.py:243
  5.9 13.5 %collective-permute-start.1 = (bf16[2,2,16,1536]{3,2,1,0:T(8,128)(2,1)S(1)}, bf16[2,2,16,1536]{3,2,1,0:T(8,128)(2,1)S(1)}, u32[]{:S(2)}, u32[]{:S(2)}) collective-permute-start(bf16[2,2,16,1536]{3,2,1,0:T(8,128)(2,1)S(1)} %maximum_bitcast_fusion.refs_0_.own), channel_id=1, source_target_pairs={{0,7},{1,0},{2,1},{3,2},{4,3},{5,4},{6,5},{7,6},{8,15},{9,8},{10,9... | collective-permute-start | bytes 589832 | tf_op jit(solution)/shard_map/ppermute | solution.py:244
  17.5 11.9 %collective-permute-start.2 = (bf16[2,2,16,1536]{3,2,1,0:T(8,128)(2,1)S(1)}, bf16[2,2,16,1536]{3,2,1,0:T(8,128)(2,1)S(1)}, u32[]{:S(2)}, u32[]{:S(2)}) collective-permute-start(bf16[2,2,16,1536]{3,2,1,0:T(8,128)(2,1)S(1)} %collective-permute-done.refs_1_), channel_id=1, source_target_pairs={{0,1},{1,2},{2,3},{3,4},{4,5},{5,6},{6,7},{7,0},{8,9},{9,10},{10,1... | collective-permute-start | bytes 589832 | tf_op jit(solution)/shard_map/ppermute | solution.py:243
  19.4 16.0 %collective-permute-start.3 = (bf16[2,2,16,1536]{3,2,1,0:T(8,128)(2,1)S(1)}, bf16[2,2,16,1536]{3,2,1,0:T(8,128)(2,1)S(1)}, u32[]{:S(2)}, u32[]{:S(2)}) collective-permute-start(bf16[2,2,16,1536]{3,2,1,0:T(8,128)(2,1)S(1)} %collective-permute-done.1.refs_2_), channel_id=1, source_target_pairs={{0,7},{1,0},{2,1},{3,2},{4,3},{5,4},{6,5},{7,6},{8,15},{9,8},{10,9... | collective-permute-start | bytes 589832 | tf_op jit(solution)/shard_map/ppermute | solution.py:244
  24.5 16.7 %collective-permute-start.6 = (bf16[2,2,16,1536]{3,2,1,0:T(8,128)(2,1)S(1)}, bf16[2,2,16,1536]{3,2,1,0:T(8,128)(2,1)S(1)}, u32[]{:S(2)}, u32[]{:S(2)}) collective-permute-start(bf16[2,2,16,1536]{3,2,1,0:T(8,128)(2,1)S(1)} %maximum_bitcast_fusion.refs_0_.own), channel_id=1, source_target_pairs={{0,4},{1,5},{2,6},{3,7},{4,0},{5,1},{6,2},{7,3},{8,12},{9,13},{10,... | collective-permute-start | bytes 589832 | tf_op jit(solution)/shard_map/ppermute | solution.py:246
  29.4 12.2 %collective-permute-start.4 = (bf16[2,2,16,1536]{3,2,1,0:T(8,128)(2,1)S(1)}, bf16[2,2,16,1536]{3,2,1,0:T(8,128)(2,1)S(1)}, u32[]{:S(2)}, u32[]{:S(2)}) collective-permute-start(bf16[2,2,16,1536]{3,2,1,0:T(8,128)(2,1)S(1)} %collective-permute-done.2.refs_3_), channel_id=1, source_target_pairs={{0,1},{1,2},{2,3},{3,4},{4,5},{5,6},{6,7},{7,0},{8,9},{9,10},{10,1... | collective-permute-start | bytes 589832 | tf_op jit(solution)/shard_map/ppermute | solution.py:243
  35.4 8.9 %collective-permute-start.5 = (bf16[2,2,16,1536]{3,2,1,0:T(8,128)(2,1)S(1)}, bf16[2,2,16,1536]{3,2,1,0:T(8,128)(2,1)S(1)}, u32[]{:S(2)}, u32[]{:S(2)}) collective-permute-start(bf16[2,2,16,1536]{3,2,1,0:T(8,128)(2,1)S(1)} %collective-permute-done.3.refs_4_), channel_id=1, source_target_pairs={{0,7},{1,0},{2,1},{3,2},{4,3},{5,4},{6,5},{7,6},{8,15},{9,8},{10,9... | collective-permute-start | bytes 589832 | tf_op jit(solution)/shard_map/ppermute | solution.py:244
  41.2 11.5 %copy-start = (bf16[27,16,256]{2,1,0:T(8,128)(2,1)S(1)}, bf16[27,16,256]{2,1,0:T(8,128)(2,1)}, u32[]{:S(2)}) copy-start(bf16[27,16,256]{2,1,0:T(8,128)(2,1)} %param.4) | copy-start | bytes 663556
  46.1 27.8 %collective-permute-start.7 = (bf16[8,2,16,1536]{3,2,1,0:T(8,128)(2,1)}, bf16[8,2,16,1536]{3,2,1,0:T(8,128)(2,1)S(1)}, u32[]{:S(2)}, u32[]{:S(2)}) collective-permute-start(bf16[8,2,16,1536]{3,2,1,0:T(8,128)(2,1)} %get-tuple-element.10), channel_id=1, source_target_pairs={{0,16},{16,0},{1,17},{17,1},{2,18},{18,2},{3,19},{19,3},{4,20},{20... | collective-permute-start | bytes 2359304 | tf_op jit(solution)/shard_map/ppermute | solution.py:257
  48.1 25.9 %collective-permute-start.8 = (bf16[8,16,1536]{2,1,0:T(8,128)(2,1)}, bf16[8,16,1536]{2,1,0:T(8,128)(2,1)S(1)}, u32[]{:S(2)}, u32[]{:S(2)}) collective-permute-start(bf16[8,16,1536]{2,1,0:T(8,128)(2,1)} %get-tuple-element.11), channel_id=1, source_target_pairs={{0,496},{16,32},{32,16},{48,64},{64,48},{80,96},{96,80},{112,128},... | collective-permute-start | bytes 1179656 | tf_op jit(solution)/shard_map/ppermute | solution.py:255
  54.2 30.2 %all-to-all-start = ((bf16[8,32,512]{2,1,0:T(8,128)(2,1)}), bf16[8,32,512]{2,1,0:T(8,128)(2,1)S(1)}, u32[]{:S(2)}, u32[]{:S(2)}) async-start(bf16[8,32,512]{2,1,0:T(8,128)(2,1)} %shard_map.61), calls=%async_computation | async-start | bytes 524288 | tf_op jit(solution)/shard_map/all_to_all | solution.py:260
  59.8 14.2 %collective-permute-start.9 = (bf16[816,128]{1,0:T(8,128)(2,1)S(1)}, bf16[816,128]{1,0:T(8,128)(2,1)S(1)}, u32[]{:S(2)}, u32[]{:S(2)}) collective-permute-start(bf16[816,128]{1,0:T(8,128)(2,1)S(1)} %shard_map.59), channel_id=1, source_target_pairs={{0,8},{8,0},{1,9},{9,1},{2,10},{10,2},{3,11},{11,3},{4,12},{12,4},... | collective-permute-start | bytes 626696 | tf_op jit(solution)/shard_map/ppermute | solution.py:249
  67.5 16.9 %collective-permute-start.11 = (bf16[8,16,1536]{2,1,0:T(8,128)(2,1)}, bf16[8,16,1536]{2,1,0:T(8,128)(2,1)}, u32[]{:S(2)}, u32[]{:S(2)}) collective-permute-start(bf16[8,16,1536]{2,1,0:T(8,128)(2,1)} %get-tuple-element.14), channel_id=1, source_target_pairs={{0,496},{16,32},{32,16},{48,64},{64,48},{80,96},{96,80},{112,128},... | collective-permute-start | bytes 1179656 | tf_op jit(solution)/shard_map/ppermute | solution.py:256
  76.7 0.7 copy-start.1
  77.4 23.7 %collective-permute-start.10 = (f32[16,3072]{1,0:T(8,128)}, f32[16,3072]{1,0:T(8,128)}, u32[]{:S(2)}, u32[]{:S(2)}) collective-permute-start(f32[16,3072]{1,0:T(8,128)} %get-tuple-element.13), channel_id=1, source_target_pairs={{0,8},{8,0},{1,9},{9,1},{2,10},{10,2},{3,11},{11,3},{4,12},{12,4},... | collective-permute-start | bytes 589832 | tf_op jit(solution)/shard_map/ppermute | solution.py:276
  88.5 31.4 %collective-permute-start.12 = (f32[16,3072]{1,0:T(8,128)}, f32[16,3072]{1,0:T(8,128)S(1)}, u32[]{:S(2)}, u32[]{:S(2)}) collective-permute-start(f32[16,3072]{1,0:T(8,128)} %get-tuple-element.16), channel_id=1, source_target_pairs={{0,8},{8,0},{1,9},{9,1},{2,10},{10,2},{3,11},{11,3},{4,12},{12,4},... | collective-permute-start | bytes 589832 | tf_op jit(solution)/shard_map/ppermute | solution.py:280
  95.0 6.1 %copy-start.2 = (f32[16,3072]{1,0:T(8,128)S(1)}, f32[16,3072]{1,0:T(8,128)}, u32[]{:S(2)}) copy-start(f32[16,3072]{1,0:T(8,128)} %copy-done.1) | copy-start | bytes 589828
  95.0 16.4 %all-to-all-start.1 = ((f32[8,4,8,432]{3,2,1,0:T(8,128)}), f32[8,4,8,432]{3,2,1,0:T(8,128)S(1)}, u32[]{:S(2)}, u32[]{:S(2)}) async-start(f32[8,4,8,432]{3,2,1,0:T(8,128)} %shard_map.63), calls=%async_computation.1 | async-start | bytes 1048576 | tf_op jit(solution)/shard_map/all_to_all | solution.py:272
  112.6 14.8 %all-to-all-start.2 = ((f32[8,8,432]{2,1,0:T(8,128)}), f32[8,8,432]{2,1,0:T(8,128)S(1)}, u32[]{:S(2)}, u32[]{:S(2)}) async-start(f32[8,8,432]{2,1,0:T(8,128)} %shard_map.64), calls=%async_computation.2 | async-start | bytes 262144 | tf_op jit(solution)/shard_map/all_to_all | solution.py:283
